TPU v7x, 32 devices: a whole 2x2x4 slice. The times are simulated.
32 devices in a mesh: parts: 2 (over x), mesh: 16 (over z, y, core).
Axes of the slice: x: 2, y: 2, z: 4, core: 2. Of those that a mesh axis runs over, the one named last changes fastest.
Arguments:
- grid_in: bfloat16 [474, 8192], P(None, ('parts', 'mesh')), parts along dimension 1, may hold values from -6 to 6
- mesh_init: bfloat16 [512, 512], P(('parts', 'mesh')), parts along dimension 0, may hold values from -6 to 6
- embed_weight: bfloat16 [474, 512], replicated, may hold values from -0.25 to 0.25
- enc_send: bfloat16 [512, 512], replicated, may hold values from -0.25 to 0.25
- enc_recv: bfloat16 [512, 512], replicated, may hold values from -0.25 to 0.25
- enc_node: bfloat16 [512, 512], replicated, may hold values from -0.25 to 0.25
- mid_send: bfloat16 [512, 512], replicated, may hold values from -0.25 to 0.25
- mid_recv: bfloat16 [512, 512], replicated, may hold values from -0.25 to 0.25
- mid_node: bfloat16 [512, 512], replicated, may hold values from -0.25 to 0.25
- dec_send: bfloat16 [512, 512], replicated, may hold values from -0.25 to 0.25
- dec_recv: bfloat16 [512, 512], replicated, may hold values from -0.25 to 0.25
- dec_node: bfloat16 [512, 512], replicated, may hold values from -0.25 to 0.25
- mid_gain: float32 [512], replicated, may hold values from 0.5 to 1.5
- cotangent: bfloat16 [8192, 512], P(('parts', 'mesh')), parts along dimension 0, may hold values from -0.035888672 to 0.035888672
- enc_from: int32 [48, 256], P('mesh'), may hold values from 0 to 255
- enc_into: int32 [48, 256], P('mesh'), may hold values from 0 to 15
- enc_count: int32 [48], P('mesh'), may hold values from 1 to 256, as said below
- mid_from: int32 [256, 32], P('mesh'), may hold values from 0 to 15
- mid_into: int32 [256, 32], P('mesh'), may hold values from 0 to 15
- mid_count: int32 [256], P('mesh'), may hold values from 0 to 32, as said below
- dec_from: int32 [48, 512], P('mesh'), may hold values from 0 to 15
- dec_into: int32 [48, 512], P('mesh'), may hold values from 0 to 255
- dec_count: int32 [48], P('mesh'), may hold values from 1 to 512, as said below
Outputs:
- update: bfloat16 [8192, 512], P(('parts', 'mesh')), parts along dimension 0
- embed_grad: float32 [948, 512], P('parts'), parts along dimension 0
- encode_grad: float32 [1024, 512], P('parts'), parts along dimension 0
- process_grad: float32 [1024, 512], P('parts'), parts along dimension 0
- decode_grad: float32 [1024, 512], P('parts'), parts along dimension 0
- output_grad: float32 [1024, 512], P('parts'), parts along dimension 0
There are 2 independent parts, one for each index of `parts`. A program takes and returns all parts, laid end to end along the dimension named above; an argument that names none is the same for every part. Nothing has to cross between parts.
Inputs may be any that keep to these rules, and one draw needn't show every extreme that they name: `enc_count`: at most 256; in every draw one destination block is full from each of its 3 neighbouring source blocks. `mid_count`: at most 32; in every draw one destination block is full from every source block. `dec_count`: at most 512; in every draw one destination block is full from each of its 3 neighbouring source blocks.
All inputs are finite; a program needn't handle non-finite values.
Results may differ from a plain program's by a relative error of at most 0.018.
Values may be sent and summed in bfloat16 or wider, within the bound.
A program may use at most 64 MiB of HBM per device.

v0:
```python
import jax
import jax.numpy as jnp
from jax import lax
from jax.sharding import PartitionSpec as P

EPSILON = 1e-05


def with_halo(cells, sides, width):
    for axis, dim in sides:
        count = lax.axis_size(axis)
        head = lax.slice_in_dim(cells, 0, width, axis=dim)
        tail = lax.slice_in_dim(cells, cells.shape[dim] - width, cells.shape[dim], axis=dim)
        cells = jnp.concatenate(
            [
                lax.ppermute(tail, axis, [(i, (i + 1) % count) for i in range(count)]),
                cells,
                lax.ppermute(head, axis, [((i + 1) % count, i) for i in range(count)]),
            ],
            axis=dim,
        )
    return cells


def shifted(shard, axis, by):
    count = lax.axis_size(axis)
    return lax.ppermute(shard, axis, [(i, (i + by) % count) for i in range(count)])


def layer_norm(values):
    center = values - jnp.mean(values, axis=-1, keepdims=True)
    spread = jnp.mean(center * center, axis=-1, keepdims=True)
    return center * lax.rsqrt(spread + EPSILON)


def silu_slope(values):
    sigma = jax.nn.sigmoid(values)
    return sigma * (1.0 + values * (1.0 - sigma))


def mm(left, right):
    return jnp.dot(left, right, preferred_element_type=jnp.float32)


def mm_right_t(left, right):
    return jnp.einsum("ae,de->ad", left, right, preferred_element_type=jnp.float32)


def mm_left_t(left, right):
    return jnp.einsum("ad,ae->de", left, right, preferred_element_type=jnp.float32)


def selector(index, valid, rows):
    flat = index.reshape(-1)
    picks = lax.broadcasted_iota(jnp.int32, (rows, flat.shape[0]), 0) == flat[None, :]
    if valid is not None:
        picks = picks & valid.reshape(-1)[None, :]
    return picks.astype(jnp.bfloat16)


def live_slots(index, count):
    return lax.broadcasted_iota(jnp.int32, index.shape, 1) < count[:, None]


def block_rows(index, rows):
    return lax.broadcasted_iota(jnp.int32, index.shape, 0) * rows + index


def collect(table, rows, shape):
    picked = jnp.einsum("rs,rd->sd", table, rows, preferred_element_type=jnp.float32)
    return picked.astype(jnp.bfloat16).reshape(shape + (rows.shape[1],))


def send_slots(block):
    return lax.all_to_all(block, "mesh", split_axis=0, concat_axis=0, tiled=True)


def margin(block):
    return with_halo(block, (("mesh", 0),), block.shape[0])


def return_margin(near_grad, rows):
    total = near_grad[rows : 2 * rows]
    for offset, piece in ((-1, near_grad[:rows]), (1, near_grad[2 * rows :])):
        total = total + shifted(piece.astype(jnp.bfloat16), "mesh", offset).astype(piece.dtype)
    return total


def edge_forward(arrived, target, table):
    width = arrived.shape[-1]
    target_at = jnp.einsum("rs,rd->sd", table, target, preferred_element_type=jnp.float32)
    inputs = arrived.reshape(-1, width).astype(jnp.float32) + target_at
    message = jax.nn.silu(inputs).astype(jnp.bfloat16)
    return (mm(table, message), inputs)


def edge_backward(grad_agg, inputs, table, shape):
    grad_at = jnp.einsum("rs,rd->sd", table, grad_agg, preferred_element_type=jnp.float32)
    grad_in = (grad_at * silu_slope(inputs)).astype(jnp.bfloat16)
    return (grad_in.reshape(shape), mm(table, grad_in))


def fetch(projected, asked):
    table = selector(asked, None, projected.shape[0])
    return (send_slots(collect(table, projected, asked.shape)), table)


def give_back(grad_slots, handle):
    width = grad_slots.shape[-1]
    returned = send_slots(grad_slots)
    return mm(handle, returned.reshape(-1, width))


def shards(
    grid_in,
    mesh_init,
    embed_weight,
    enc_send,
    enc_recv,
    enc_node,
    mid_send,
    mid_recv,
    mid_node,
    dec_send,
    dec_recv,
    dec_node,
    mid_gain,
    cotangent,
    enc_from,
    enc_into,
    enc_count,
    mid_from,
    mid_into,
    mid_count,
    dec_from,
    dec_into,
    dec_count,
):
    grid_rows = grid_in.shape[1]
    mesh_rows = mesh_init.shape[0]
    mid_asked = lax.all_to_all(mid_from, "mesh", split_axis=0, concat_axis=0, tiled=True)
    pre_act = jnp.einsum("cg,cd->gd", grid_in, embed_weight, preferred_element_type=jnp.float32)
    hidden = jax.nn.silu(pre_act).astype(jnp.bfloat16)
    enc_proj = mm(hidden, enc_send).astype(jnp.bfloat16)
    enc_near = margin(enc_proj)
    enc_source = selector(block_rows(enc_from, grid_rows), None, enc_near.shape[0])
    enc_arrived = collect(enc_source, enc_near, enc_from.shape)
    enc_table = selector(enc_into, live_slots(enc_into, enc_count), mesh_rows)
    enc_target = mm(mesh_init, enc_recv).astype(jnp.bfloat16)
    enc_agg, enc_inputs = edge_forward(enc_arrived, enc_target, enc_table)
    enc_norm = layer_norm(enc_agg).astype(jnp.bfloat16)
    latent = (mesh_init.astype(jnp.float32) + mm(enc_norm, enc_node)).astype(jnp.bfloat16)
    mid_proj = mm(latent, mid_send).astype(jnp.bfloat16)
    mid_target = mm(latent, mid_recv).astype(jnp.bfloat16)
    mid_arrived, mid_handle = fetch(mid_proj, mid_asked)
    mid_table = selector(mid_into, live_slots(mid_into, mid_count), mesh_rows)
    mid_agg, mid_inputs = edge_forward(mid_arrived, mid_target, mid_table)
    mid_norm = (layer_norm(mid_agg) * mid_gain).astype(jnp.bfloat16)
    latent_two = (latent.astype(jnp.float32) + mm(mid_norm, mid_node)).astype(jnp.bfloat16)
    dec_proj = mm(latent_two, dec_send).astype(jnp.bfloat16)
    dec_target = mm(hidden, dec_recv).astype(jnp.bfloat16)
    dec_near = margin(dec_proj)
    dec_source = selector(block_rows(dec_from, mesh_rows), None, dec_near.shape[0])
    dec_arrived = collect(dec_source, dec_near, dec_from.shape)
    dec_table = selector(dec_into, live_slots(dec_into, dec_count), grid_rows)
    dec_agg, dec_inputs = edge_forward(dec_arrived, dec_target, dec_table)
    dec_norm = layer_norm(dec_agg).astype(jnp.bfloat16)
    update = (hidden.astype(jnp.float32) + mm(dec_norm, dec_node)).astype(jnp.bfloat16)
    output_term = mm_left_t(dec_norm, cotangent)
    pull = jax.vjp(layer_norm, dec_agg)[1]
    dec_cot = pull(mm_right_t(cotangent, dec_node))[0].astype(jnp.bfloat16)
    dec_slots, dec_dst_sum = edge_backward(dec_cot, dec_inputs, dec_table, dec_arrived.shape)
    dec_near_grad = mm(dec_source, dec_slots.reshape(-1, dec_slots.shape[-1]))
    dec_src_grad = return_margin(dec_near_grad, mesh_rows).astype(jnp.bfloat16)
    dec_dst_grad = dec_dst_sum.astype(jnp.bfloat16)
    decode_term = mm_left_t(latent_two, dec_src_grad)
    latent_two_grad = mm_right_t(dec_src_grad, dec_send)
    pull = jax.vjp(lambda values: layer_norm(values) * mid_gain, mid_agg)[1]
    mid_cot = pull(mm_right_t(latent_two_grad.astype(jnp.bfloat16), mid_node))[0].astype(
        jnp.bfloat16
    )
    mid_slots, mid_dst_sum = edge_backward(mid_cot, mid_inputs, mid_table, mid_arrived.shape)
    mid_src_grad = give_back(mid_slots, mid_handle).astype(jnp.bfloat16)
    mid_dst_grad = mid_dst_sum.astype(jnp.bfloat16)
    process_term = mm_left_t(latent, mid_src_grad)
    latent_grad = (
        latent_two_grad + mm_right_t(mid_src_grad, mid_send) + mm_right_t(mid_dst_grad, mid_recv)
    ).astype(jnp.bfloat16)
    pull = jax.vjp(layer_norm, enc_agg)[1]
    enc_cot = pull(mm_right_t(latent_grad, enc_node))[0].astype(jnp.bfloat16)
    enc_slots, enc_dst_sum = edge_backward(enc_cot, enc_inputs, enc_table, enc_arrived.shape)
    enc_near_grad = mm(enc_source, enc_slots.reshape(-1, enc_slots.shape[-1]))
    enc_src_grad = return_margin(enc_near_grad, grid_rows).astype(jnp.bfloat16)
    encode_term = mm_left_t(hidden, enc_src_grad)
    hidden_grad = (
        cotangent.astype(jnp.float32)
        + mm_right_t(enc_src_grad, enc_send)
        + mm_right_t(dec_dst_grad, dec_recv)
    )
    pre_grad = (hidden_grad * silu_slope(pre_act)).astype(jnp.bfloat16)
    embed_term = jnp.einsum("cg,gd->cd", grid_in, pre_grad, preferred_element_type=jnp.float32)
    embed_grad, encode_grad, process_grad, decode_grad, output_grad = lax.psum(
        (embed_term, encode_term, process_term, decode_term, output_term), "mesh"
    )
    return (update, embed_grad, encode_grad, process_grad, decode_grad, output_grad)


def solution(mesh):
    placed = (
        P(None, ("parts", "mesh")),
        P(("parts", "mesh"), None),
        P(),
        P(),
        P(),
        P(),
        P(),
        P(),
        P(),
        P(),
        P(),
        P(),
        P(),
        P(("parts", "mesh"), None),
        P("mesh", None),
        P("mesh", None),
        P("mesh"),
        P("mesh", None),
        P("mesh", None),
        P("mesh"),
        P("mesh", None),
        P("mesh", None),
        P("mesh"),
    )
    return jax.shard_map(
        shards,
        mesh=mesh,
        in_specs=placed,
        out_specs=(
            P(("parts", "mesh"), None),
            P("parts", None),
            P("parts", None),
            P("parts", None),
            P("parts", None),
            P("parts", None),
        ),
        check_vma=False,
    )
```

profile of v0, /device:TPU:0, one launch (start us, length us, event | category | flops | bytes accessed | tf_op | source)
XLA Modules:
  0.0 256.2 jit_solution(13624631593324874992)
XLA Ops:
  7.2 2.4 multiply_convert_fusion.7
  9.9 5.5 %collective-permute-start.1 = (bf16[256,512]{1,0:T(8,128)(2,1)S(1)}, bf16[256,512]{1,0:T(8,128)(2,1)S(1)}, u32[]{:S(2)}, u32[]{:S(2)}) collective-permute-start(bf16[256,512]{1,0:T(8,128)(2,1)S(1)} %convolution_convert_fusion.3), channel_id=1, source_target_pairs={{1,0},{2,1},{3,2},{4,3},{5,4},{6,5},{7,6},{8,7},{9,8},{10,9},{11,1... | collective-permute-start | bytes 786440 | tf_op jit(solution)/shard_map/ppermute | solution.py:18
  15.5 5.8 %all-to-all-start = ((s32[16,1,32]{2,1,0:T(1,128)}), s32[16,1,32]{2,1,0:T(1,128)S(1)}, u32[]{:S(2)}, u32[]{:S(2)}) async-start(s32[16,1,32]{2,1,0:T(1,128)} %bitcast), calls=%async_computation | async-start | bytes 16384 | tf_op jit(solution)/shard_map/all_to_all | solution.py:141
  22.1 5.6 %all-to-all-done = s32[16,1,32]{2,1,0:T(1,128)S(1)} async-done(((s32[16,1,32]{2,1,0:T(1,128)}), s32[16,1,32]{2,1,0:T(1,128)S(1)}, u32[]{:S(2)}, u32[]{:S(2)}) %all-to-all-start) | async-done | bytes 2080 | tf_op jit(solution)/shard_map/all_to_all | solution.py:141
  28.2 0.7 reduce.3
  28.9 1.8 convert_add_fusion.1
  30.8 0.6 fusion.125
  32.5 1.3 convolution_convert_fusion.1
  33.8 3.6 %all-to-all-start.1 = ((bf16[16,32,512]{2,1,0:T(8,128)(2,1)}), bf16[16,32,512]{2,1,0:T(8,128)(2,1)S(1)}, u32[]{:S(2)}, u32[]{:S(2)}) async-start(bf16[16,32,512]{2,1,0:T(8,128)(2,1)} %bitcast.1), calls=%async_computation.1 | async-start | bytes 1048576 | tf_op jit(solution)/shard_map/all_to_all | solution.py:75
  37.8 2.5 fusion.9
  40.3 11.3 %all-to-all-done.1 = bf16[16,32,512]{2,1,0:T(8,128)(2,1)S(1)} async-done(((bf16[16,32,512]{2,1,0:T(8,128)(2,1)}), bf16[16,32,512]{2,1,0:T(8,128)(2,1)S(1)}, u32[]{:S(2)}, u32[]{:S(2)}) %all-to-all-start.1) | async-done | bytes 524320 | tf_op jit(solution)/shard_map/all_to_all | solution.py:75
  51.6 1.4 convolution_add_fusion
  53.1 1.8 fusion.126
  55.6 0.6 copy-done.56
  56.6 2.7 %collective-permute-start.3 = (bf16[16,512]{1,0:T(8,128)(2,1)S(1)}, bf16[16,512]{1,0:T(8,128)(2,1)S(1)}, u32[]{:S(2)}, u32[]{:S(2)}) collective-permute-start(bf16[16,512]{1,0:T(8,128)(2,1)S(1)} %convolution_convert_fusion.6), channel_id=1, source_target_pairs={{1,0},{2,1},{3,2},{4,3},{5,4},{6,5},{7,6},{8,7},{9,8},{10,9},{11,1... | collective-permute-start | bytes 49160 | tf_op jit(solution)/shard_map/ppermute | solution.py:18
  59.4 1.3 collective-permute-done.3
  60.8 4.4 %collective-permute-done.2 = bf16[16,512]{1,0:T(8,128)(2,1)S(1)} collective-permute-done((bf16[16,512]{1,0:T(8,128)(2,1)S(1)}, bf16[16,512]{1,0:T(8,128)(2,1)S(1)}, u32[]{:S(2)}, u32[]{:S(2)}) %collective-permute-start.2) | collective-permute-done | bytes 16416 | tf_op jit(solution)/shard_map/ppermute | solution.py:16
  65.2 2.5 convert_add_fusion
  67.7 1.3 fusion.127
  70.1 1.5 fusion
  72.6 0.9 collective-permute-done.4
  73.5 4.5 %collective-permute-done.5 = bf16[16,512]{1,0:T(8,128)(2,1)S(1)} collective-permute-done((bf16[16,512]{1,0:T(8,128)(2,1)S(1)}, bf16[16,512]{1,0:T(8,128)(2,1)S(1)}, u32[]{:S(2)}, u32[]{:S(2)}) %collective-permute-start.5) | collective-permute-done | bytes 16416 | tf_op jit(solution)/shard_map/ppermute | solution.py:27
  78.9 1.3 fusion.12
  80.3 3.7 %all-to-all-start.2 = ((bf16[16,32,512]{2,1,0:T(8,128)(2,1)}), bf16[16,32,512]{2,1,0:T(8,128)(2,1)S(1)}, u32[]{:S(2)}, u32[]{:S(2)}) async-start(bf16[16,32,512]{2,1,0:T(8,128)(2,1)} %bitcast.3), calls=%async_computation.2 | async-start | bytes 1048576 | tf_op jit(solution)/shard_map/all_to_all | solution.py:75
  84.3 1.4 fusion.119
  85.7 3.1 %fusion.23 = f32[256,512]{1,0:T(8,128)} fusion(bf16[512,512]{1,0:T(8,128)(2,1)S(1)} %copy-done, bf16[1536,512]{1,0:T(8,128)(2,1)} %copy-done.9, s32[1536]{0:T(1024)S(1)} %copy-done.23, pred[1536]{0:T(1024)(128)(4,1)S(1)} %copy-done.36), kind=kOutput, calls=%fused_computation.35 | convolution fusion | flops 537788416 | bytes 2629120 | tf_op jit(solution)/shard_map/ae,de->ad/dot_general | solution.py:46
  88.8 2.0 fusion.30
  90.8 7.4 %all-to-all-done.2 = bf16[16,32,512]{2,1,0:T(8,128)(2,1)S(1)} async-done(((bf16[16,32,512]{2,1,0:T(8,128)(2,1)}), bf16[16,32,512]{2,1,0:T(8,128)(2,1)S(1)}, u32[]{:S(2)}, u32[]{:S(2)}) %all-to-all-start.2) | async-done | bytes 524320 | tf_op jit(solution)/shard_map/all_to_all | solution.py:75
  98.4 1.3 multiply_reduce_fusion.2
  100.0 3.9 %fusion.129 = (bf16[768,512]{1,0:T(8,128)(2,1)S(1)}, f32[768,512]{1,0:T(8,128)}) fusion(f32[768,512]{1,0:T(8,128)} %copy-done.66, s32[768]{0:T(1024)S(1)} %copy-done.34, pred[768]{0:T(1024)(128)(4,1)S(1)} %copy-done.49, f32[16,512]{1,0:T(8,128)S(1)} %get-tuple-element.14, f32[16]{0:T(128)S(1)} %negate_multiply_fusion.1, s32[768]{0:T(1024)S(1)} %copy-done.53), kind=kOutput, calls=%fused_computation.178 | convolution fusion | flops 621125632 | bytes 3971904 | tf_op jit(solution)/shard_map/dot_general | solution.py:42
  103.9 2.8 %collective-permute-start.6 = (bf16[256,512]{1,0:T(8,128)(2,1)S(1)}, bf16[256,512]{1,0:T(8,128)(2,1)S(1)}, u32[]{:S(2)}, u32[]{:S(2)}) collective-permute-start(bf16[256,512]{1,0:T(8,128)(2,1)S(1)} %get-tuple-element.19), channel_id=1, source_target_pairs={{0,15},{1,0},{2,1},{3,2},{4,3},{5,4},{6,5},{7,6},{8,7},{9,8},{10,9... | collective-permute-start | bytes 786440 | tf_op jit(solution)/shard_map/ppermute | solution.py:27
  106.7 1.3 fusion.135
  108.0 1.3 fusion.134
  109.3 1.3 collective-permute-done.6
  110.6 4.6 %collective-permute-done.7 = bf16[256,512]{1,0:T(8,128)(2,1)S(1)} collective-permute-done((bf16[256,512]{1,0:T(8,128)(2,1)S(1)}, bf16[256,512]{1,0:T(8,128)(2,1)S(1)}, u32[]{:S(2)}, u32[]{:S(2)}) %collective-permute-start.7) | collective-permute-done | bytes 262176 | tf_op jit(solution)/shard_map/ppermute | solution.py:27
  115.2 1.1 fusion.50
  116.3 1.3 fusion.133
  117.6 2.8 %convolution_bitcast_fusion = f32[474,512]{1,0:T(8,128)} fusion(bf16[474,256]{1,0:T(8,128)(2,1)S(1)} %copy-done.64, f32[256,512]{1,0:T(8,128)} %fusion.23, bf16[256,512]{1,0:T(8,128)(2,1)S(1)} %fusion.50, bf16[512,512]{1,0:T(8,128)(2,1)S(1)} %copy-done.19, f32[256,512]{1,0:T(8,128)} %get-tuple-element.26, bf16[256,512]{1,0:T(8,128)(2,1)S(1)} %copy-done.17), kind=kOutput, calls=%fused_computation.21 | convolution fusion | flops 260046848 | bytes 3310592 | tf_op jit(solution)/shard_map/cg,gd->cd/dot_general | solution.py:201
  120.5 1.0 copy-done.6
  121.5 1.0 fusion.15
  122.6 119.3 %all-reduce.3.cloned.1.call-done = (f32[474,512]{1,0:T(8,128)}, f32[512,512]{1,0:T(8,128)}, f32[512,512]{1,0:T(8,128)}, f32[512,512]{1,0:T(8,128)}, f32[512,512]{1,0:T(8,128)}) async-done(((f32[474,512]{1,0:T(8,128)}, f32[512,512]{1,0:T(8,128)}, f32[512,512]{1,0:T(8,128)}, f32[512,512]{1,0:T(8,128)}, f32[512,512]{1,0:T(8,128)}), (f32[474,512]{1,0:T(8,128)}, f32[512,512]{1,0:T(8,128)}, f32[512,512]{1,0:T(8,128)}, ...) | async-done | bytes 5165072 | tf_op jit(solution)/shard_map/psum | solution.py:202
  241.9 2.4 copy.34
  244.2 1.0 copy.35
  245.2 1.0 copy.36
  246.2 0.6 copy-done.12
  246.8 1.0 copy.37
  247.8 0.6 copy-done.11
  248.4 1.0 copy.38
  (185 shorter events, 7.9 us)
Async XLA Ops:
  7.2 30.6 %copy-start = (bf16[512,512]{1,0:T(8,128)(2,1)S(1)}, bf16[512,512]{1,0:T(8,128)(2,1)}, u32[]{:S(2)}) copy-start(bf16[512,512]{1,0:T(8,128)(2,1)} %param.33) | copy-start | bytes 1572868
  7.2 14.1 %copy-start.65 = (s32[3]{0:T(128)S(1)}, s32[3]{0:T(128)}, u32[]{:S(2)}) copy-start(s32[3]{0:T(128)} %param.39) | copy-start | bytes 40
  7.2 14.2 %copy-start.50 = (s32[3,256]{1,0:T(4,128)S(1)}, s32[3,256]{1,0:T(4,128)}, u32[]{:S(2)}) copy-start(s32[3,256]{1,0:T(4,128)} %param.38) | copy-start | bytes 9220
  7.2 14.2 %copy-start.21 = (bf16[16,512]{1,0:T(8,128)(2,1)S(1)}, bf16[16,512]{1,0:T(8,128)(2,1)}, u32[]{:S(2)}) copy-start(bf16[16,512]{1,0:T(8,128)(2,1)} %param.24) | copy-start | bytes 49156
  7.2 14.2 %copy-start.20 = (bf16[512,512]{1,0:T(8,128)(2,1)S(1)}, bf16[512,512]{1,0:T(8,128)(2,1)}, u32[]{:S(2)}) copy-start(bf16[512,512]{1,0:T(8,128)(2,1)} %param.27) | copy-start | bytes 1572868
  9.6 12.4 %copy-start.51 = (s32[3,256]{1,0:T(4,128)S(1)}, s32[3,256]{1,0:T(4,128)}, u32[]{:S(2)}) copy-start(s32[3,256]{1,0:T(4,128)} %param.37) | copy-start | bytes 9220
  9.9 19.0 %collective-permute-start.1 = (bf16[256,512]{1,0:T(8,128)(2,1)S(1)}, bf16[256,512]{1,0:T(8,128)(2,1)S(1)}, u32[]{:S(2)}, u32[]{:S(2)}) collective-permute-start(bf16[256,512]{1,0:T(8,128)(2,1)S(1)} %convolution_convert_fusion.3), channel_id=1, source_target_pairs={{1,0},{2,1},{3,2},{4,3},{5,4},{6,5},{7,6},{8,7},{9,8},{10,9},{11,1... | collective-permute-start | bytes 786440 | tf_op jit(solution)/shard_map/ppermute | solution.py:18
  15.5 13.5 %collective-permute-start = (bf16[256,512]{1,0:T(8,128)(2,1)S(1)}, bf16[256,512]{1,0:T(8,128)(2,1)}, u32[]{:S(2)}, u32[]{:S(2)}) collective-permute-start(bf16[256,512]{1,0:T(8,128)(2,1)S(1)} %convolution_convert_fusion.3), channel_id=1, source_target_pairs={{0,1},{1,2},{2,3},{3,4},{4,5},{5,6},{6,7},{7,8},{8,9},{9,10},{10,1... | collective-permute-start | bytes 786440 | tf_op jit(solution)/shard_map/ppermute | solution.py:16
  15.5 12.2 %all-to-all-start = ((s32[16,1,32]{2,1,0:T(1,128)}), s32[16,1,32]{2,1,0:T(1,128)S(1)}, u32[]{:S(2)}, u32[]{:S(2)}) async-start(s32[16,1,32]{2,1,0:T(1,128)} %bitcast), calls=%async_computation | async-start | bytes 16384 | tf_op jit(solution)/shard_map/all_to_all | solution.py:141
  21.4 9.3 %copy-start.48 = (pred[768]{0:T(1024)(128)(4,1)}, pred[768]{0:T(1024)(128)(4,1)S(1)}, u32[]{:S(2)}) copy-start(pred[768]{0:T(1024)(128)(4,1)S(1)} %lt.50) | copy-start | bytes 2308
  21.4 9.3 %copy-start.33 = (s32[768]{0:T(1024)}, s32[768]{0:T(1024)S(1)}, u32[]{:S(2)}) copy-start(s32[768]{0:T(1024)S(1)} %eq.66) | copy-start | bytes 9220
  22.1 8.7 %copy-start.52 = (s32[768]{0:T(1024)}, s32[768]{0:T(1024)S(1)}, u32[]{:S(2)}) copy-start(s32[768]{0:T(1024)S(1)} %eq.69) | copy-start | bytes 9220
  31.9 5.6 %copy-start.62 = (s32[16]{0:T(128)S(1)}, s32[16]{0:T(128)}, u32[]{:S(2)}) copy-start(s32[16]{0:T(128)} %param.42) | copy-start | bytes 196
  31.9 5.7 %copy-start.63 = (s32[3]{0:T(128)S(1)}, s32[3]{0:T(128)}, u32[]{:S(2)}) copy-start(s32[3]{0:T(128)} %param.45) | copy-start | bytes 40
  31.9 5.8 %copy-start.44 = (s32[3,512]{1,0:T(4,128)S(1)}, s32[3,512]{1,0:T(4,128)}, u32[]{:S(2)}) copy-start(s32[3,512]{1,0:T(4,128)} %param.44) | copy-start | bytes 18436
  33.8 17.8 %all-to-all-start.1 = ((bf16[16,32,512]{2,1,0:T(8,128)(2,1)}), bf16[16,32,512]{2,1,0:T(8,128)(2,1)S(1)}, u32[]{:S(2)}, u32[]{:S(2)}) async-start(bf16[16,32,512]{2,1,0:T(8,128)(2,1)} %bitcast.1), calls=%async_computation.1 | async-start | bytes 1048576 | tf_op jit(solution)/shard_map/all_to_all | solution.py:75
  37.5 15.6 %copy-start.28 = (s32[512]{0:T(512)}, s32[512]{0:T(512)S(1)}, u32[]{:S(2)}) copy-start(s32[512]{0:T(512)S(1)} %eq.72) | copy-start | bytes 6148
  37.6 15.4 %copy-start.46 = (pred[512]{0:T(512)(128)(4,1)}, pred[512]{0:T(512)(128)(4,1)S(1)}, u32[]{:S(2)}) copy-start(pred[512]{0:T(512)(128)(4,1)S(1)} %lt.53) | copy-start | bytes 1540
  37.7 32.4 %copy-start.35 = (pred[1536]{0:T(1024)(128)(4,1)}, pred[1536]{0:T(1024)(128)(4,1)S(1)}, u32[]{:S(2)}) copy-start(pred[1536]{0:T(1024)(128)(4,1)S(1)} %lt.47) | copy-start | bytes 4612
  37.7 32.3 %copy-start.22 = (s32[1536]{0:T(1024)}, s32[1536]{0:T(1024)S(1)}, u32[]{:S(2)}) copy-start(s32[1536]{0:T(1024)S(1)} %eq.60) | copy-start | bytes 18436
  37.8 13.8 %copy-start.7 = (bf16[512,512]{1,0:T(8,128)(2,1)S(1)}, bf16[512,512]{1,0:T(8,128)(2,1)}, u32[]{:S(2)}) copy-start(bf16[512,512]{1,0:T(8,128)(2,1)} %param.30) | copy-start | bytes 1572868
  53.1 6.3 %copy-start.45 = (s32[3,512]{1,0:T(4,128)S(1)}, s32[3,512]{1,0:T(4,128)}, u32[]{:S(2)}) copy-start(s32[3,512]{1,0:T(4,128)} %param.43) | copy-start | bytes 18436
  56.6 4.2 %collective-permute-start.3 = (bf16[16,512]{1,0:T(8,128)(2,1)S(1)}, bf16[16,512]{1,0:T(8,128)(2,1)S(1)}, u32[]{:S(2)}, u32[]{:S(2)}) collective-permute-start(bf16[16,512]{1,0:T(8,128)(2,1)S(1)} %convolution_convert_fusion.6), channel_id=1, source_target_pairs={{1,0},{2,1},{3,2},{4,3},{5,4},{6,5},{7,6},{8,7},{9,8},{10,9},{11,1... | collective-permute-start | bytes 49160 | tf_op jit(solution)/shard_map/ppermute | solution.py:18
  59.3 5.9 %collective-permute-start.2 = (bf16[16,512]{1,0:T(8,128)(2,1)S(1)}, bf16[16,512]{1,0:T(8,128)(2,1)S(1)}, u32[]{:S(2)}, u32[]{:S(2)}) collective-permute-start(bf16[16,512]{1,0:T(8,128)(2,1)S(1)} %convolution_convert_fusion.6), channel_id=1, source_target_pairs={{0,1},{1,2},{2,3},{3,4},{4,5},{5,6},{6,7},{7,8},{8,9},{9,10},{10,1... | collective-permute-start | bytes 49160 | tf_op jit(solution)/shard_map/ppermute | solution.py:16
  71.6 7.3 %copy-start.9 = (bf16[1536,512]{1,0:T(8,128)(2,1)}, bf16[1536,512]{1,0:T(8,128)(2,1)S(1)}, u32[]{:S(2)}) copy-start(bf16[1536,512]{1,0:T(8,128)(2,1)S(1)} %fusion) | copy-start | bytes 4718596
  71.6 6.7 %copy-start.38 = (f32[512]{0:T(512)S(1)}, f32[512]{0:T(512)}, u32[]{:S(2)}) copy-start(f32[512]{0:T(512)} %param.35) | copy-start | bytes 6148
  71.6 6.7 %copy-start.42 = (f32[16]{0:T(128)S(1)}, f32[16]{0:T(128)}, u32[]{:S(2)}) copy-start(f32[16]{0:T(128)} %copy-done.41) | copy-start | bytes 196
  71.6 7.0 %copy-start.61 = (f32[16]{0:T(128)S(1)}, f32[16]{0:T(128)}, u32[]{:S(2)}) copy-start(f32[16]{0:T(128)} %copy-done.60) | copy-start | bytes 196
  71.6 7.1 %copy-start.57 = (f32[16]{0:T(128)S(1)}, f32[16]{0:T(128)}, u32[]{:S(2)}) copy-start(f32[16]{0:T(128)} %copy-done.56) | copy-start | bytes 196
  71.6 7.3 %copy-start.10 = (f32[512,512]{1,0:T(8,128)S(1)}, f32[512,512]{1,0:T(8,128)}, u32[]{:S(2)}) copy-start(f32[512,512]{1,0:T(8,128)} %convolution_add_fusion) | copy-start | bytes 3145732
  71.6 7.3 %copy-start.29 = (s32[512]{0:T(512)S(1)}, s32[512]{0:T(512)}, u32[]{:S(2)}) copy-start(s32[512]{0:T(512)} %copy-done.28) | copy-start | bytes 6148
  71.6 7.3 %copy-start.47 = (pred[512]{0:T(512)(128)(4,1)S(1)}, pred[512]{0:T(512)(128)(4,1)}, u32[]{:S(2)}) copy-start(pred[512]{0:T(512)(128)(4,1)} %copy-done.46) | copy-start | bytes 1540
  72.0 1.5 collective-permute-start.4
  72.1 5.9 %collective-permute-start.5 = (bf16[16,512]{1,0:T(8,128)(2,1)S(1)}, bf16[16,512]{1,0:T(8,128)(2,1)S(1)}, u32[]{:S(2)}, u32[]{:S(2)}) collective-permute-start(bf16[16,512]{1,0:T(8,128)(2,1)S(1)} %get-tuple-element.22), channel_id=1, source_target_pairs={{0,1},{1,2},{2,3},{3,4},{4,5},{5,6},{6,7},{7,8},{8,9},{9,10},{10,1... | collective-permute-start | bytes 49160 | tf_op jit(solution)/shard_map/ppermute | solution.py:27
  80.3 17.9 %all-to-all-start.2 = ((bf16[16,32,512]{2,1,0:T(8,128)(2,1)}), bf16[16,32,512]{2,1,0:T(8,128)(2,1)S(1)}, u32[]{:S(2)}, u32[]{:S(2)}) async-start(bf16[16,32,512]{2,1,0:T(8,128)(2,1)} %bitcast.3), calls=%async_computation.2 | async-start | bytes 1048576 | tf_op jit(solution)/shard_map/all_to_all | solution.py:75
  84.0 157.9 %all-reduce.3.cloned.1.call-start = ((), (), s32[]{:S(2)}) async-start(), calls=%async_computation.3 | async-start | bytes 10354688 | tf_op jit(solution)/shard_map/psum | solution.py:202
  85.7 12.6 %copy-start.27 = (s32[512]{0:T(512)S(1)}, s32[512]{0:T(512)}, u32[]{:S(2)}) copy-start(s32[512]{0:T(512)} %copy-done.26) | copy-start | bytes 6148
  88.8 11.2 %copy-start.34 = (s32[768]{0:T(1024)S(1)}, s32[768]{0:T(1024)}, u32[]{:S(2)}) copy-start(s32[768]{0:T(1024)} %copy-done.33) | copy-start | bytes 9220
  90.8 8.9 %copy-start.59 = (f32[16]{0:T(128)S(1)}, f32[16]{0:T(128)}, u32[]{:S(2)}) copy-start(f32[16]{0:T(128)} %copy-done.58) | copy-start | bytes 196
  90.8 9.0 %copy-start.40 = (f32[16]{0:T(128)S(1)}, f32[16]{0:T(128)}, u32[]{:S(2)}) copy-start(f32[16]{0:T(128)} %copy-done.39) | copy-start | bytes 196
  90.8 9.0 %copy-start.55 = (f32[16]{0:T(128)S(1)}, f32[16]{0:T(128)}, u32[]{:S(2)}) copy-start(f32[16]{0:T(128)} %copy-done.54) | copy-start | bytes 196
  90.8 9.2 %copy-start.49 = (pred[768]{0:T(1024)(128)(4,1)S(1)}, pred[768]{0:T(1024)(128)(4,1)}, u32[]{:S(2)}) copy-start(pred[768]{0:T(1024)(128)(4,1)} %copy-done.48) | copy-start | bytes 2308
  90.8 9.2 %copy-start.53 = (s32[768]{0:T(1024)S(1)}, s32[768]{0:T(1024)}, u32[]{:S(2)}) copy-start(s32[768]{0:T(1024)} %copy-done.52) | copy-start | bytes 9220
  103.9 6.6 %collective-permute-start.6 = (bf16[256,512]{1,0:T(8,128)(2,1)S(1)}, bf16[256,512]{1,0:T(8,128)(2,1)S(1)}, u32[]{:S(2)}, u32[]{:S(2)}) collective-permute-start(bf16[256,512]{1,0:T(8,128)(2,1)S(1)} %get-tuple-element.19), channel_id=1, source_target_pairs={{0,15},{1,0},{2,1},{3,2},{4,3},{5,4},{6,5},{7,6},{8,7},{9,8},{10,9... | collective-permute-start | bytes 786440 | tf_op jit(solution)/shard_map/ppermute | solution.py:27
  106.7 8.5 %collective-permute-start.7 = (bf16[256,512]{1,0:T(8,128)(2,1)S(1)}, bf16[256,512]{1,0:T(8,128)(2,1)S(1)}, u32[]{:S(2)}, u32[]{:S(2)}) collective-permute-start(bf16[256,512]{1,0:T(8,128)(2,1)S(1)} %get-tuple-element.20), channel_id=1, source_target_pairs={{0,1},{1,2},{2,3},{3,4},{4,5},{5,6},{6,7},{7,8},{8,9},{9,10},{10,1... | collective-permute-start | bytes 786440 | tf_op jit(solution)/shard_map/ppermute | solution.py:27
  109.3 8.4 %copy-start.17 = (bf16[256,512]{1,0:T(8,128)(2,1)S(1)}, bf16[256,512]{1,0:T(8,128)(2,1)}, u32[]{:S(2)}) copy-start(bf16[256,512]{1,0:T(8,128)(2,1)} %param.36) | copy-start | bytes 786436
  109.3 8.4 %copy-start.19 = (bf16[512,512]{1,0:T(8,128)(2,1)S(1)}, bf16[512,512]{1,0:T(8,128)(2,1)}, u32[]{:S(2)}) copy-start(bf16[512,512]{1,0:T(8,128)(2,1)} %param.26) | copy-start | bytes 1572868
  110.6 7.1 %copy-start.64 = (bf16[474,256]{1,0:T(8,128)(2,1)S(1)}, bf16[474,256]{1,0:T(8,128)(2,1)}, u32[]{:S(2)}) copy-start(bf16[474,256]{1,0:T(8,128)(2,1)} %param.23) | copy-start | bytes 728068
  (31 other events, 82.9 us)
Sparse Core Ops, SparseCore 0:
  120.6 121.2 all-reduce.2
where the time goes:
time: 257 us; the launch traced here: 256 us
  waiting for transfers between devices  161 us (63%)
  matrix products  40.9 us (16%)
  starting transfers between devices  24.9 us (10%)
  between operations  14.8 us (6%)
  local copies, waits for them, and re-layouts  11.7 us (5%)
  other arithmetic  3.28 us (1%)
    psum x1, waiting for transfers between devices, shards(): lax.psum((embed_term, encode_term, process_term, decode_term, output_term...  119 us
    all_to_all x2, waiting for transfers between devices, send_slots(): lax.all_to_all(block, 'mesh', split_axis=0, concat_axis=0, tiled=True)  18.7 us
    ppermute x4, waiting for transfers between devices, shifted(): lax.ppermute(shard, axis, [(i, (i + by) % count) for i in range(count)])  11.3 us
    unnamed x139, local copies, waits for them, and re-layouts  10.8 us
    dot_general x11, matrix products, mm(): return jnp.dot(left, right, preferred_element_type=jnp.float32)  10.1 us
    ppermute x2, starting transfers between devices, with_halo(): lax.ppermute(head, axis, [((i + 1) % count, i) for i in range(count)])  8.24 us
    dot_general x6, matrix products, mm_right_t(): jnp.einsum('ae,de->ad', left, right, preferred_element_type=jnp.float32)  7.47 us
    all_to_all x2, starting transfers between devices, send_slots(): lax.all_to_all(block, 'mesh', split_axis=0, concat_axis=0, tiled=True)  7.29 us
  transfers between devices with their start and end apart: 12, of which 10 were waited for; matrix products, arithmetic and copies ran while one was open for 6% of the time, Pallas kernels for 0%

commit v1 on v0

--- a/solution.py
+++ b/solution.py
@@ -109,6 +109,14 @@
     width = grad_slots.shape[-1]
     returned = send_slots(grad_slots)
     return mm(handle, returned.reshape(-1, width))
+
+
+def whole_rows(block):
+    return lax.all_gather(block, "mesh", axis=0, tiled=True)
+
+
+def summed(term):
+    return lax.psum(term.astype(jnp.bfloat16), "mesh").astype(jnp.float32)
 
 
 def shards(
@@ -173,7 +181,6 @@
     dec_near_grad = mm(dec_source, dec_slots.reshape(-1, dec_slots.shape[-1]))
     dec_src_grad = return_margin(dec_near_grad, mesh_rows).astype(jnp.bfloat16)
     dec_dst_grad = dec_dst_sum.astype(jnp.bfloat16)
-    decode_term = mm_left_t(latent_two, dec_src_grad)
     latent_two_grad = mm_right_t(dec_src_grad, dec_send)
     pull = jax.vjp(lambda values: layer_norm(values) * mid_gain, mid_agg)[1]
     mid_cot = pull(mm_right_t(latent_two_grad.astype(jnp.bfloat16), mid_node))[0].astype(
@@ -182,7 +189,6 @@
     mid_slots, mid_dst_sum = edge_backward(mid_cot, mid_inputs, mid_table, mid_arrived.shape)
     mid_src_grad = give_back(mid_slots, mid_handle).astype(jnp.bfloat16)
     mid_dst_grad = mid_dst_sum.astype(jnp.bfloat16)
-    process_term = mm_left_t(latent, mid_src_grad)
     latent_grad = (
         latent_two_grad + mm_right_t(mid_src_grad, mid_send) + mm_right_t(mid_dst_grad, mid_recv)
     ).astype(jnp.bfloat16)
@@ -199,9 +205,11 @@
     )
     pre_grad = (hidden_grad * silu_slope(pre_act)).astype(jnp.bfloat16)
     embed_term = jnp.einsum("cg,gd->cd", grid_in, pre_grad, preferred_element_type=jnp.float32)
-    embed_grad, encode_grad, process_grad, decode_grad, output_grad = lax.psum(
-        (embed_term, encode_term, process_term, decode_term, output_term), "mesh"
-    )
+    process_grad = mm_left_t(whole_rows(latent), whole_rows(mid_src_grad))
+    decode_grad = mm_left_t(whole_rows(latent_two), whole_rows(dec_src_grad))
+    output_grad = summed(output_term)
+    encode_grad = summed(encode_term)
+    embed_grad = summed(embed_term)
     return (update, embed_grad, encode_grad, process_grad, decode_grad, output_grad)
 
 

time: 257 us -> 261 us (1.016)
  blocking collectives: 0 us -> 86.7 us
  waiting for transfers between devices: 161 us -> 85.2 us
  local copies, waits for them, and re-layouts: 11.7 us -> 2.08 us
  other arithmetic: 3.28 us -> 7.68 us
  matrix products: 40.9 us -> 37.8 us
    all_gather x0 -> x4, blocking collectives: none -> 86.7 us  [whole_rows(): return lax.all_gather(block, 'mesh', axis=0, tiled=True)]
    psum x1, waiting for transfers between devices: 119 us -> 53.7 us  [summed(): return lax.psum(term.astype(jnp.bfloat16), 'mesh').astype(jnp.float32)]
    unnamed x139 -> x148, local copies, waits for them, and re-layouts: 10.8 us -> 1.21 us
    all_to_all x2, waiting for transfers between devices: 18.7 us -> 11.3 us  [send_slots(): lax.all_to_all(block, 'mesh', split_axis=0, concat_axis=0, tiled=True)]
    convert_element_type x0 -> x3, other arithmetic: none -> 4.39 us  [summed(): return lax.psum(term.astype(jnp.bfloat16), 'mesh').astype(jnp.float32)]
    ppermute x2, waiting for transfers between devices: 4.42 us -> 1.32 us  [with_halo(): lax.ppermute(tail, axis, [(i, (i + 1) % count) for i in range(count)])]
  transfers between devices with their start and end apart: 12 -> 12, of which waited for: 10 -> 8; matrix products, arithmetic and copies ran while one was open for 6% -> 5% of each run, Pallas kernels for 0% -> 0%
where the time goes in v1:
time: 261 us; the launch traced here: 260 us
  blocking collectives  86.7 us (33%)
  waiting for transfers between devices  85.2 us (33%)
  matrix products  37.8 us (14%)
  starting transfers between devices  26 us (10%)
  between operations  14.9 us (6%)
  other arithmetic  7.68 us (3%)
    all_gather x4, blocking collectives, whole_rows(): return lax.all_gather(block, 'mesh', axis=0, tiled=True)  86.7 us
    psum x1, waiting for transfers between devices, summed(): return lax.psum(term.astype(jnp.bfloat16), 'mesh').astype(jnp.float32)  53.7 us
    ppermute x4, waiting for transfers between devices, shifted(): lax.ppermute(shard, axis, [(i, (i + by) % count) for i in range(count)])  13.1 us
    all_to_all x2, waiting for transfers between devices, send_slots(): lax.all_to_all(block, 'mesh', split_axis=0, concat_axis=0, tiled=True)  11.3 us
    dot_general x11, matrix products, mm(): return jnp.dot(left, right, preferred_element_type=jnp.float32)  10.2 us
    ppermute x2, starting transfers between devices, with_halo(): lax.ppermute(head, axis, [((i + 1) % count, i) for i in range(count)])  9.36 us
    all_to_all x2, starting transfers between devices, send_slots(): lax.all_to_all(block, 'mesh', split_axis=0, concat_axis=0, tiled=True)  7.29 us
    dot_general x6, matrix products, mm_right_t(): jnp.einsum('ae,de->ad', left, right, preferred_element_type=jnp.float32)  6.05 us
  transfers between devices with their start and end apart: 12, of which 8 were waited for; matrix products, arithmetic and copies ran while one was open for 5% of the time, Pallas kernels for 0%

profile of v1, /device:TPU:0, one launch (start us, length us, event | category | flops | bytes accessed | tf_op | source)
XLA Modules:
  0.0 260.4 jit_solution(18222111503634587033)
XLA Ops:
  7.2 2.4 multiply_convert_fusion.7
  9.9 0.5 collective-permute-start
  10.5 5.0 %collective-permute-start.1 = (bf16[256,512]{1,0:T(8,128)(2,1)S(1)}, bf16[256,512]{1,0:T(8,128)(2,1)}, u32[]{:S(2)}, u32[]{:S(2)}) collective-permute-start(bf16[256,512]{1,0:T(8,128)(2,1)S(1)} %convolution_convert_fusion.6), channel_id=1, source_target_pairs={{1,0},{2,1},{3,2},{4,3},{5,4},{6,5},{7,6},{8,7},{9,8},{10,9},{11,1... | collective-permute-start | bytes 786440 | tf_op jit(solution)/shard_map/ppermute | solution.py:18
  15.5 3.6 %all-to-all-start = ((s32[16,1,32]{2,1,0:T(1,128)}), s32[16,1,32]{2,1,0:T(1,128)S(1)}, u32[]{:S(2)}, u32[]{:S(2)}) async-start(s32[16,1,32]{2,1,0:T(1,128)} %bitcast), calls=%async_computation | async-start | bytes 16384 | tf_op jit(solution)/shard_map/all_to_all | solution.py:149
  19.3 0.5 fusion.30
  19.9 5.6 %all-to-all-done = s32[16,1,32]{2,1,0:T(1,128)S(1)} async-done(((s32[16,1,32]{2,1,0:T(1,128)}), s32[16,1,32]{2,1,0:T(1,128)S(1)}, u32[]{:S(2)}, u32[]{:S(2)}) %all-to-all-start) | async-done | bytes 2080 | tf_op jit(solution)/shard_map/all_to_all | solution.py:149
  25.5 0.5 broadcast.200
  26.0 0.7 reduce.3
  26.8 1.8 convert_add_fusion.1
  28.6 0.6 fusion.125
  29.5 0.6 copy-done.63
  30.4 1.2 convolution_convert_fusion.3
  31.6 3.6 %all-to-all-start.1 = ((bf16[16,32,512]{2,1,0:T(8,128)(2,1)}), bf16[16,32,512]{2,1,0:T(8,128)(2,1)S(1)}, u32[]{:S(2)}, u32[]{:S(2)}) async-start(bf16[16,32,512]{2,1,0:T(8,128)(2,1)} %bitcast.1), calls=%async_computation.1 | async-start | bytes 1048576 | tf_op jit(solution)/shard_map/all_to_all | solution.py:75
  35.6 2.5 fusion.9
  38.1 11.3 %all-to-all-done.1 = bf16[16,32,512]{2,1,0:T(8,128)(2,1)S(1)} async-done(((bf16[16,32,512]{2,1,0:T(8,128)(2,1)}), bf16[16,32,512]{2,1,0:T(8,128)(2,1)S(1)}, u32[]{:S(2)}, u32[]{:S(2)}) %all-to-all-start.1) | async-done | bytes 524320 | tf_op jit(solution)/shard_map/all_to_all | solution.py:75
  49.4 1.4 convolution_add_fusion
  50.9 1.8 fusion.126
  53.5 4.3 %collective-permute-start.3 = (bf16[16,512]{1,0:T(8,128)(2,1)S(1)}, bf16[16,512]{1,0:T(8,128)(2,1)S(1)}, u32[]{:S(2)}, u32[]{:S(2)}) collective-permute-start(bf16[16,512]{1,0:T(8,128)(2,1)S(1)} %convolution_convert_fusion.9), channel_id=1, source_target_pairs={{1,0},{2,1},{3,2},{4,3},{5,4},{6,5},{7,6},{8,7},{9,8},{10,9},{11,1... | collective-permute-start | bytes 49160 | tf_op jit(solution)/shard_map/ppermute | solution.py:18
  57.9 1.3 collective-permute-done.2
  59.3 2.5 convert_add_fusion
  61.8 1.3 fusion.127
  64.2 1.5 fusion
  66.1 4.5 %collective-permute-start.4 = (bf16[16,512]{1,0:T(8,128)(2,1)S(1)}, bf16[16,512]{1,0:T(8,128)(2,1)S(1)}, u32[]{:S(2)}, u32[]{:S(2)}) collective-permute-start(bf16[16,512]{1,0:T(8,128)(2,1)S(1)} %get-tuple-element.19), channel_id=1, source_target_pairs={{0,15},{1,0},{2,1},{3,2},{4,3},{5,4},{6,5},{7,6},{8,7},{9,8},{10,9... | collective-permute-start | bytes 49160 | tf_op jit(solution)/shard_map/ppermute | solution.py:27
  70.6 1.4 collective-permute-done.4
  72.0 4.4 %collective-permute-done.5 = bf16[16,512]{1,0:T(8,128)(2,1)S(1)} collective-permute-done((bf16[16,512]{1,0:T(8,128)(2,1)S(1)}, bf16[16,512]{1,0:T(8,128)(2,1)S(1)}, u32[]{:S(2)}, u32[]{:S(2)}) %collective-permute-start.5) | collective-permute-done | bytes 16416 | tf_op jit(solution)/shard_map/ppermute | solution.py:27
  77.4 1.3 fusion.12
  78.7 3.7 %all-to-all-start.2 = ((bf16[16,32,512]{2,1,0:T(8,128)(2,1)}), bf16[16,32,512]{2,1,0:T(8,128)(2,1)S(1)}, u32[]{:S(2)}, u32[]{:S(2)}) async-start(bf16[16,32,512]{2,1,0:T(8,128)(2,1)} %bitcast.3), calls=%async_computation.2 | async-start | bytes 1048576 | tf_op jit(solution)/shard_map/all_to_all | solution.py:75
  82.5 27.2 %all_gather.12 = bf16[256,512]{1,0:T(8,128)(2,1)} all-gather(bf16[16,512]{1,0:T(8,128)(2,1)S(1)} %fusion.27), channel_id=1, replica_groups=mesh['parts'=2,'mesh'=16] {'mesh'}, dimensions={0}, use_global_device_ids=true | all-gather | bytes 278528 | tf_op jit(solution)/shard_map/all_gather | solution.py:115
  109.6 21.1 %all_gather.14 = bf16[256,512]{1,0:T(8,128)(2,1)} all-gather(bf16[16,512]{1,0:T(8,128)(2,1)S(1)} %fusion.28), channel_id=1, replica_groups=mesh['parts'=2,'mesh'=16] {'mesh'}, dimensions={0}, use_global_device_ids=true | all-gather | bytes 278528 | tf_op jit(solution)/shard_map/all_gather | solution.py:115
  130.7 1.2 convolution_convert_fusion.1
  132.0 3.1 %fusion.24 = f32[256,512]{1,0:T(8,128)} fusion(bf16[512,512]{1,0:T(8,128)(2,1)S(1)} %copy-done, bf16[1536,512]{1,0:T(8,128)(2,1)} %copy-done.9, s32[1536]{0:T(1024)S(1)} %copy-done.25, pred[1536]{0:T(1024)(128)(4,1)S(1)} %copy-done.40), kind=kOutput, calls=%fused_computation.38 | convolution fusion | flops 537788416 | bytes 2629120 | tf_op jit(solution)/shard_map/ae,de->ad/dot_general | solution.py:46
  135.1 1.4 fusion.31
  136.7 0.6 multiply_reduce_fusion.2
  137.5 4.0 %fusion.129 = (bf16[768,512]{1,0:T(8,128)(2,1)S(1)}, f32[768,512]{1,0:T(8,128)}) fusion(f32[768,512]{1,0:T(8,128)} %copy-done.71, s32[768]{0:T(1024)S(1)} %copy-done.38, pred[768]{0:T(1024)(128)(4,1)S(1)} %copy-done.54, f32[16,512]{1,0:T(8,128)S(1)} %get-tuple-element.12, f32[16]{0:T(128)S(1)} %negate_multiply_fusion.1, s32[768]{0:T(1024)S(1)} %copy-done.58), kind=kOutput, calls=%fused_computation.180 | convolution fusion | flops 621125632 | bytes 3971904 | tf_op jit(solution)/shard_map/dot_general | solution.py:42
  142.1 1.0 fusion.16
  143.2 2.6 collective-permute-done.6
  145.8 4.7 %collective-permute-done.7 = bf16[256,512]{1,0:T(8,128)(2,1)S(1)} collective-permute-done((bf16[256,512]{1,0:T(8,128)(2,1)S(1)}, bf16[256,512]{1,0:T(8,128)(2,1)S(1)}, u32[]{:S(2)}, u32[]{:S(2)}) %collective-permute-start.7) | collective-permute-done | bytes 262176 | tf_op jit(solution)/shard_map/ppermute | solution.py:27
  150.5 1.2 fusion.51
  151.6 1.1 convolution_convert_fusion.2
  152.8 1.5 fusion.15
  154.3 19.7 %all_gather.15 = bf16[256,512]{1,0:T(8,128)(2,1)S(1)} all-gather(bf16[16,512]{1,0:T(8,128)(2,1)S(1)} %fusion.74), channel_id=1, replica_groups=mesh['parts'=2,'mesh'=16] {'mesh'}, dimensions={0}, use_global_device_ids=true | all-gather | bytes 278528 | tf_op jit(solution)/shard_map/all_gather | solution.py:115
  174.0 1.3 fusion.134
  175.3 18.8 %all_gather.13 = bf16[256,512]{1,0:T(8,128)(2,1)S(1)} all-gather(bf16[16,512]{1,0:T(8,128)(2,1)S(1)} %convolution_convert_fusion.8), channel_id=1, replica_groups=mesh['parts'=2,'mesh'=16] {'mesh'}, dimensions={0}, use_global_device_ids=true | all-gather | bytes 278528 | tf_op jit(solution)/shard_map/all_gather | solution.py:115
  194.1 1.3 fusion.133
  195.4 53.7 %all-reduce.3.cloned.1.call-done = (bf16[474,512]{1,0:T(8,128)(2,1)}, bf16[512,512]{1,0:T(8,128)(2,1)}, bf16[512,512]{1,0:T(8,128)(2,1)}) async-done(((bf16[474,512]{1,0:T(8,128)(2,1)}, bf16[512,512]{1,0:T(8,128)(2,1)}, bf16[512,512]{1,0:T(8,128)(2,1)}), (bf16[474,512]{1,0:T(8,128)(2,1)}, bf16[512,512]{1,0:T(8,128)(2,1)}, bf16[512,512]{1,0:T(8,128)(2,1)})) %all-reduce.3.cloned.1.call-update) | async-done | bytes 1533968 | tf_op jit(solution)/shard_map/psum | solution.py:119
  249.1 2.2 convert_element_type.215
  251.4 1.1 convert_element_type.217
  252.5 1.1 convert_element_type.213
  (201 shorter events, 5.8 us)
Async XLA Ops:
  7.2 28.4 %copy-start = (bf16[512,512]{1,0:T(8,128)(2,1)S(1)}, bf16[512,512]{1,0:T(8,128)(2,1)}, u32[]{:S(2)}) copy-start(bf16[512,512]{1,0:T(8,128)(2,1)} %param.33) | copy-start | bytes 1572868
  7.2 11.9 %copy-start.55 = (s32[3,256]{1,0:T(4,128)S(1)}, s32[3,256]{1,0:T(4,128)}, u32[]{:S(2)}) copy-start(s32[3,256]{1,0:T(4,128)} %param.38) | copy-start | bytes 9220
  7.2 12.0 %copy-start.70 = (s32[3]{0:T(128)S(1)}, s32[3]{0:T(128)}, u32[]{:S(2)}) copy-start(s32[3]{0:T(128)} %param.39) | copy-start | bytes 40
  7.2 12.1 %copy-start.23 = (bf16[16,512]{1,0:T(8,128)(2,1)S(1)}, bf16[16,512]{1,0:T(8,128)(2,1)}, u32[]{:S(2)}) copy-start(bf16[16,512]{1,0:T(8,128)(2,1)} %param.24) | copy-start | bytes 49156
  7.2 12.1 %copy-start.19 = (bf16[512,512]{1,0:T(8,128)(2,1)S(1)}, bf16[512,512]{1,0:T(8,128)(2,1)}, u32[]{:S(2)}) copy-start(bf16[512,512]{1,0:T(8,128)(2,1)} %param.27) | copy-start | bytes 1572868
  9.6 10.2 %copy-start.56 = (s32[3,256]{1,0:T(4,128)S(1)}, s32[3,256]{1,0:T(4,128)}, u32[]{:S(2)}) copy-start(s32[3,256]{1,0:T(4,128)} %param.37) | copy-start | bytes 9220
  9.9 16.9 %collective-permute-start = (bf16[256,512]{1,0:T(8,128)(2,1)S(1)}, bf16[256,512]{1,0:T(8,128)(2,1)S(1)}, u32[]{:S(2)}, u32[]{:S(2)}) collective-permute-start(bf16[256,512]{1,0:T(8,128)(2,1)S(1)} %convolution_convert_fusion.6), channel_id=1, source_target_pairs={{0,1},{1,2},{2,3},{3,4},{4,5},{5,6},{6,7},{7,8},{8,9},{9,10},{10,1... | collective-permute-start | bytes 786440 | tf_op jit(solution)/shard_map/ppermute | solution.py:16
  10.5 16.3 %collective-permute-start.1 = (bf16[256,512]{1,0:T(8,128)(2,1)S(1)}, bf16[256,512]{1,0:T(8,128)(2,1)}, u32[]{:S(2)}, u32[]{:S(2)}) collective-permute-start(bf16[256,512]{1,0:T(8,128)(2,1)S(1)} %convolution_convert_fusion.6), channel_id=1, source_target_pairs={{1,0},{2,1},{3,2},{4,3},{5,4},{6,5},{7,6},{8,7},{9,8},{10,9},{11,1... | collective-permute-start | bytes 786440 | tf_op jit(solution)/shard_map/ppermute | solution.py:18
  15.5 10.0 %all-to-all-start = ((s32[16,1,32]{2,1,0:T(1,128)}), s32[16,1,32]{2,1,0:T(1,128)S(1)}, u32[]{:S(2)}, u32[]{:S(2)}) async-start(s32[16,1,32]{2,1,0:T(1,128)} %bitcast), calls=%async_computation | async-start | bytes 16384 | tf_op jit(solution)/shard_map/all_to_all | solution.py:149
  19.2 9.4 %copy-start.37 = (s32[768]{0:T(1024)}, s32[768]{0:T(1024)S(1)}, u32[]{:S(2)}) copy-start(s32[768]{0:T(1024)S(1)} %eq.66) | copy-start | bytes 9220
  19.3 9.3 %copy-start.53 = (pred[768]{0:T(1024)(128)(4,1)}, pred[768]{0:T(1024)(128)(4,1)S(1)}, u32[]{:S(2)}) copy-start(pred[768]{0:T(1024)(128)(4,1)S(1)} %lt.50) | copy-start | bytes 2308
  19.9 8.7 %copy-start.57 = (s32[768]{0:T(1024)}, s32[768]{0:T(1024)S(1)}, u32[]{:S(2)}) copy-start(s32[768]{0:T(1024)S(1)} %eq.69) | copy-start | bytes 9220
  29.3 8.8 %copy-start.43 = (f32[16]{0:T(128)}, f32[16]{0:T(128)S(1)}, u32[]{:S(2)}) copy-start(f32[16]{0:T(128)S(1)} %broadcast_multiply_fusion.2) | copy-start | bytes 196
  31.6 17.8 %all-to-all-start.1 = ((bf16[16,32,512]{2,1,0:T(8,128)(2,1)}), bf16[16,32,512]{2,1,0:T(8,128)(2,1)S(1)}, u32[]{:S(2)}, u32[]{:S(2)}) async-start(bf16[16,32,512]{2,1,0:T(8,128)(2,1)} %bitcast.1), calls=%async_computation.1 | async-start | bytes 1048576 | tf_op jit(solution)/shard_map/all_to_all | solution.py:75
  35.4 15.5 %copy-start.50 = (pred[512]{0:T(512)(128)(4,1)}, pred[512]{0:T(512)(128)(4,1)S(1)}, u32[]{:S(2)}) copy-start(pred[512]{0:T(512)(128)(4,1)S(1)} %lt.53) | copy-start | bytes 1540
  35.5 15.4 %copy-start.31 = (s32[512]{0:T(512)}, s32[512]{0:T(512)S(1)}, u32[]{:S(2)}) copy-start(s32[512]{0:T(512)S(1)} %eq.72) | copy-start | bytes 6148
  35.5 28.4 %copy-start.24 = (s32[1536]{0:T(1024)}, s32[1536]{0:T(1024)S(1)}, u32[]{:S(2)}) copy-start(s32[1536]{0:T(1024)S(1)} %eq.60) | copy-start | bytes 18436
  35.6 28.3 %copy-start.39 = (pred[1536]{0:T(1024)(128)(4,1)}, pred[1536]{0:T(1024)(128)(4,1)S(1)}, u32[]{:S(2)}) copy-start(pred[1536]{0:T(1024)(128)(4,1)S(1)} %lt.47) | copy-start | bytes 4612
  35.6 13.8 %copy-start.7 = (bf16[512,512]{1,0:T(8,128)(2,1)S(1)}, bf16[512,512]{1,0:T(8,128)(2,1)}, u32[]{:S(2)}) copy-start(bf16[512,512]{1,0:T(8,128)(2,1)} %param.30) | copy-start | bytes 1572868
  50.9 6.9 %copy-start.49 = (s32[3,512]{1,0:T(4,128)S(1)}, s32[3,512]{1,0:T(4,128)}, u32[]{:S(2)}) copy-start(s32[3,512]{1,0:T(4,128)} %param.43) | copy-start | bytes 18436
  53.4 5.9 %collective-permute-start.2 = (bf16[16,512]{1,0:T(8,128)(2,1)S(1)}, bf16[16,512]{1,0:T(8,128)(2,1)S(1)}, u32[]{:S(2)}, u32[]{:S(2)}) collective-permute-start(bf16[16,512]{1,0:T(8,128)(2,1)S(1)} %convolution_convert_fusion.9), channel_id=1, source_target_pairs={{0,1},{1,2},{2,3},{3,4},{4,5},{5,6},{6,7},{7,8},{8,9},{9,10},{10,1... | collective-permute-start | bytes 49160 | tf_op jit(solution)/shard_map/ppermute | solution.py:16
  53.5 5.8 %collective-permute-start.3 = (bf16[16,512]{1,0:T(8,128)(2,1)S(1)}, bf16[16,512]{1,0:T(8,128)(2,1)S(1)}, u32[]{:S(2)}, u32[]{:S(2)}) collective-permute-start(bf16[16,512]{1,0:T(8,128)(2,1)S(1)} %convolution_convert_fusion.9), channel_id=1, source_target_pairs={{1,0},{2,1},{3,2},{4,3},{5,4},{6,5},{7,6},{8,7},{9,8},{10,9},{11,1... | collective-permute-start | bytes 49160 | tf_op jit(solution)/shard_map/ppermute | solution.py:18
  65.7 11.6 %copy-start.9 = (bf16[1536,512]{1,0:T(8,128)(2,1)}, bf16[1536,512]{1,0:T(8,128)(2,1)S(1)}, u32[]{:S(2)}) copy-start(bf16[1536,512]{1,0:T(8,128)(2,1)S(1)} %fusion) | copy-start | bytes 4718596
  65.7 11.0 %copy-start.42 = (f32[512]{0:T(512)S(1)}, f32[512]{0:T(512)}, u32[]{:S(2)}) copy-start(f32[512]{0:T(512)} %param.35) | copy-start | bytes 6148
  65.7 11.0 %copy-start.46 = (f32[16]{0:T(128)S(1)}, f32[16]{0:T(128)}, u32[]{:S(2)}) copy-start(f32[16]{0:T(128)} %copy-done.45) | copy-start | bytes 196
  65.7 11.4 %copy-start.66 = (f32[16]{0:T(128)S(1)}, f32[16]{0:T(128)}, u32[]{:S(2)}) copy-start(f32[16]{0:T(128)} %copy-done.65) | copy-start | bytes 196
  65.7 11.4 %copy-start.62 = (f32[16]{0:T(128)S(1)}, f32[16]{0:T(128)}, u32[]{:S(2)}) copy-start(f32[16]{0:T(128)} %copy-done.61) | copy-start | bytes 196
  65.7 11.6 %copy-start.10 = (f32[512,512]{1,0:T(8,128)S(1)}, f32[512,512]{1,0:T(8,128)}, u32[]{:S(2)}) copy-start(f32[512,512]{1,0:T(8,128)} %convolution_add_fusion) | copy-start | bytes 3145732
  65.7 11.6 %copy-start.32 = (s32[512]{0:T(512)S(1)}, s32[512]{0:T(512)}, u32[]{:S(2)}) copy-start(s32[512]{0:T(512)} %copy-done.31) | copy-start | bytes 6148
  65.8 11.6 %copy-start.51 = (pred[512]{0:T(512)(128)(4,1)S(1)}, pred[512]{0:T(512)(128)(4,1)}, u32[]{:S(2)}) copy-start(pred[512]{0:T(512)(128)(4,1)} %copy-done.50) | copy-start | bytes 1540
  66.1 5.9 %collective-permute-start.4 = (bf16[16,512]{1,0:T(8,128)(2,1)S(1)}, bf16[16,512]{1,0:T(8,128)(2,1)S(1)}, u32[]{:S(2)}, u32[]{:S(2)}) collective-permute-start(bf16[16,512]{1,0:T(8,128)(2,1)S(1)} %get-tuple-element.19), channel_id=1, source_target_pairs={{0,15},{1,0},{2,1},{3,2},{4,3},{5,4},{6,5},{7,6},{8,7},{9,8},{10,9... | collective-permute-start | bytes 49160 | tf_op jit(solution)/shard_map/ppermute | solution.py:27
  70.6 5.9 %collective-permute-start.5 = (bf16[16,512]{1,0:T(8,128)(2,1)S(1)}, bf16[16,512]{1,0:T(8,128)(2,1)S(1)}, u32[]{:S(2)}, u32[]{:S(2)}) collective-permute-start(bf16[16,512]{1,0:T(8,128)(2,1)S(1)} %get-tuple-element.20), channel_id=1, source_target_pairs={{0,1},{1,2},{2,3},{3,4},{4,5},{5,6},{6,7},{7,8},{8,9},{9,10},{10,1... | collective-permute-start | bytes 49160 | tf_op jit(solution)/shard_map/ppermute | solution.py:27
  78.7 52.0 %copy-start.12 = (bf16[256,512]{1,0:T(8,128)(2,1)S(1)}, bf16[256,512]{1,0:T(8,128)(2,1)}, u32[]{:S(2)}) copy-start(bf16[256,512]{1,0:T(8,128)(2,1)} %param.36) | copy-start | bytes 786436
  78.7 52.0 %copy-start.27 = (f32[256]{0:T(256)S(1)}, f32[256]{0:T(256)}, u32[]{:S(2)}) copy-start(f32[256]{0:T(256)} %copy-done.26) | copy-start | bytes 3076
  78.7 52.0 %copy-start.35 = (f32[256]{0:T(256)S(1)}, f32[256]{0:T(256)}, u32[]{:S(2)}) copy-start(f32[256]{0:T(256)} %copy-done.34) | copy-start | bytes 3076
  78.7 53.3 %copy-start.25 = (s32[1536]{0:T(1024)S(1)}, s32[1536]{0:T(1024)}, u32[]{:S(2)}) copy-start(s32[1536]{0:T(1024)} %copy-done.24) | copy-start | bytes 18436
  78.7 53.3 %copy-start.40 = (pred[1536]{0:T(1024)(128)(4,1)S(1)}, pred[1536]{0:T(1024)(128)(4,1)}, u32[]{:S(2)}) copy-start(pred[1536]{0:T(1024)(128)(4,1)} %copy-done.39) | copy-start | bytes 4612
  78.7 57.8 %all-to-all-start.2 = ((bf16[16,32,512]{2,1,0:T(8,128)(2,1)}), bf16[16,32,512]{2,1,0:T(8,128)(2,1)S(1)}, u32[]{:S(2)}, u32[]{:S(2)}) async-start(bf16[16,32,512]{2,1,0:T(8,128)(2,1)} %bitcast.3), calls=%async_computation.2 | async-start | bytes 1048576 | tf_op jit(solution)/shard_map/all_to_all | solution.py:75
  82.4 166.7 %all-reduce.3.cloned.1.call-start = ((), (), s32[]{:S(2)}) async-start(), calls=%async_computation.3 | async-start | bytes 3080192 | tf_op jit(solution)/shard_map/psum | solution.py:119
  141.5 4.2 %collective-permute-start.6 = (bf16[256,512]{1,0:T(8,128)(2,1)S(1)}, bf16[256,512]{1,0:T(8,128)(2,1)S(1)}, u32[]{:S(2)}, u32[]{:S(2)}) collective-permute-start(bf16[256,512]{1,0:T(8,128)(2,1)S(1)} %get-tuple-element.17), channel_id=1, source_target_pairs={{0,15},{1,0},{2,1},{3,2},{4,3},{5,4},{6,5},{7,6},{8,7},{9,8},{10,9... | collective-permute-start | bytes 786440 | tf_op jit(solution)/shard_map/ppermute | solution.py:27
  141.9 8.6 %collective-permute-start.7 = (bf16[256,512]{1,0:T(8,128)(2,1)S(1)}, bf16[256,512]{1,0:T(8,128)(2,1)S(1)}, u32[]{:S(2)}, u32[]{:S(2)}) collective-permute-start(bf16[256,512]{1,0:T(8,128)(2,1)S(1)} %get-tuple-element.18), channel_id=1, source_target_pairs={{0,1},{1,2},{2,3},{3,4},{4,5},{5,6},{6,7},{7,8},{8,9},{9,10},{10,1... | collective-permute-start | bytes 786440 | tf_op jit(solution)/shard_map/ppermute | solution.py:27
  143.2 9.6 %copy-start.13 = (bf16[256,512]{1,0:T(8,128)(2,1)S(1)}, bf16[256,512]{1,0:T(8,128)(2,1)}, u32[]{:S(2)}) copy-start(bf16[256,512]{1,0:T(8,128)(2,1)} %param.36) | copy-start | bytes 786436
  143.2 9.6 %copy-start.18 = (bf16[512,512]{1,0:T(8,128)(2,1)S(1)}, bf16[512,512]{1,0:T(8,128)(2,1)}, u32[]{:S(2)}) copy-start(bf16[512,512]{1,0:T(8,128)(2,1)} %param.26) | copy-start | bytes 1572868
  143.2 9.6 %copy-start.69 = (bf16[474,256]{1,0:T(8,128)(2,1)S(1)}, bf16[474,256]{1,0:T(8,128)(2,1)}, u32[]{:S(2)}) copy-start(bf16[474,256]{1,0:T(8,128)(2,1)} %param.23) | copy-start | bytes 728068
  143.2 9.6 %copy-start.72 = (f32[256,512]{1,0:T(8,128)S(1)}, f32[256,512]{1,0:T(8,128)}, u32[]{:S(2)}) copy-start(f32[256,512]{1,0:T(8,128)} %fusion.24) | copy-start | bytes 1572868
  143.2 9.6 %copy-start.73 = (f32[256,512]{1,0:T(8,128)S(1)}, f32[256,512]{1,0:T(8,128)}, u32[]{:S(2)}) copy-start(f32[256,512]{1,0:T(8,128)} %get-tuple-element.24) | copy-start | bytes 1572868
  154.2 19.8 %copy-start.15 = (bf16[256,512]{1,0:T(8,128)(2,1)S(1)}, bf16[256,512]{1,0:T(8,128)(2,1)}, u32[]{:S(2)}) copy-start(bf16[256,512]{1,0:T(8,128)(2,1)} %all_gather.14) | copy-start | bytes 786436
  154.2 39.9 %copy-start.14 = (bf16[256,512]{1,0:T(8,128)(2,1)S(1)}, bf16[256,512]{1,0:T(8,128)(2,1)}, u32[]{:S(2)}) copy-start(bf16[256,512]{1,0:T(8,128)(2,1)} %all_gather.12) | copy-start | bytes 786436
  (38 other events, 105.3 us)
Sparse Core Ops, SparseCore 0:
  154.4 94.7 all-reduce.2

commit v2 on v0

v2 whole, which is shorter than its diff:
```python
import functools

import jax
import jax.numpy as jnp
from jax import lax
from jax.experimental import pallas as pl
from jax.experimental.pallas import tpu as pltpu
from jax.sharding import PartitionSpec as P

EPSILON = 1e-05
F32 = jnp.float32
BF16 = jnp.bfloat16


def dot(left, right, dims):
    return lax.dot_general(left, right, (dims, ((), ())), preferred_element_type=F32)


def mm(left, right):
    return dot(left, right, ((1,), (0,)))


def mm_right_t(left, right):
    return dot(left, right, ((1,), (1,)))


def mm_left_t(left, right):
    return dot(left, right, ((0,), (0,)))


def normed(values):
    center = values - jnp.mean(values, axis=-1, keepdims=True)
    scale = lax.rsqrt(jnp.mean(center * center, axis=-1, keepdims=True) + EPSILON)
    return center * scale, scale


def norm_pull(unit, scale, grad):
    inner = jnp.mean(grad * unit, axis=-1, keepdims=True)
    return scale * (grad - jnp.mean(grad, axis=-1, keepdims=True) - unit * inner)


def sigmoid(values):
    return 1.0 / (1.0 + jnp.exp(-values))


def silu(values):
    return values * sigmoid(values)


def silu_slope(values):
    sigma = sigmoid(values)
    return sigma * (1.0 + values * (1.0 - sigma))


def picks(index, rows):
    places = lax.broadcasted_iota(jnp.int32, (rows, index.shape[1]), 0)
    return jnp.where(places == index, 1.0, 0.0).astype(BF16)


def kernel(
    n,
    shard,
    grid_in,
    mesh_init,
    embed_weight,
    enc_send,
    enc_recv,
    enc_node,
    mid_send,
    mid_recv,
    mid_node,
    dec_send,
    dec_recv,
    dec_node,
    mid_gain,
    cotangent,
    enc_pack,
    mid_pack,
    dec_pack,
    update,
    embed_grad,
    encode_grad,
    process_grad,
    decode_grad,
    output_grad,
    pre_act,
    hidden,
    enc_proj,
    dec_target,
    packs,
    targets,
    enc_inputs,
    agg_parts,
    agg_near,
    lat_all,
    mid_inputs,
    lat2_all,
    dec_near,
    dec_inputs,
    dec_cot,
    dec_parts,
    dec_back,
    dec_dst,
    dsg_all,
    mid_parts,
    mid_back,
    msg_all,
    cots,
    enc_src,
    terms,
    halves,
    paired,
    arrived,
    whole,
    held_grad,
    held_dst,
    near_send,
    near_recv,
    all_send,
    all_recv,
    pair_sem,
    ring_send,
    ring_recv,
):
    me = lax.axis_index("mesh")
    left = lax.rem(me + n - 1, n)
    right = lax.rem(me + 1, n)
    core = lax.rem(me, 2)
    chip = me // 2
    chips = n // 2
    partner = me + 1 - 2 * core
    grid_rows = hidden.shape[0]
    mesh_rows, width = mesh_init.shape

    def remote(src, dst, send, recv, device):
        return pltpu.make_async_remote_copy(
            src_ref=src,
            dst_ref=dst,
            send_sem=send,
            recv_sem=recv,
            device_id={"mesh": device},
            device_id_type=pl.DeviceIdType.MESH,
        )

    def to_left(which, src, dst):
        return remote(src, dst, near_send.at[which, 0], near_recv.at[which, 1], left)

    def to_right(which, src, dst):
        return remote(src, dst, near_send.at[which, 1], near_recv.at[which, 0], right)

    def near_arrive(which, first, second):
        remote(first, first, near_send.at[which, 1], near_recv.at[which, 0], right).wait_recv()
        remote(second, second, near_send.at[which, 0], near_recv.at[which, 1], left).wait_recv()

    def gather_copy(which, table, owner, peer):
        return remote(
            table.at[owner], table.at[owner], all_send.at[which, peer], all_recv.at[which, owner], peer
        )

    def gather_start(which, table):
        @pl.loop(1, n)
        def _(step):
            gather_copy(which, table, me, lax.rem(me + step, n)).start()

    def gather_take(which, table, first, last):
        @pl.loop(first, last)
        def _(step):
            owner = lax.rem(me + step, n)
            gather_copy(which, table, owner, owner).wait_recv()

    def gather_sent(which, table):
        @pl.loop(1, n)
        def _(step):
            gather_copy(which, table, me, lax.rem(me + step, n)).wait_send()

    def pair_copy(k):
        return remote(terms.at[k, 1 - core], halves.at[k], pair_sem.at[k, 0], pair_sem.at[k, 1], partner)

    def ring_copy(k, src, dst, stage, peer, slot):
        return remote(src, dst, ring_send.at[k, stage, peer], ring_recv.at[k, stage, slot], 2 * peer + core)

    def put_term(k, value):
        rows = value.shape[0]
        value = value.astype(BF16)
        for o in range(n):
            low, high = o * shard, min((o + 1) * shard, rows)
            if high - low < shard:
                terms[k, o % 2, o // 2] = jnp.zeros((shard, width), BF16)
            if low < high:
                terms[k, o % 2, o // 2, 0 : high - low] = value[low:high]
        pair_copy(k).start()

    def scatter_start(k):
        pair_copy(k).wait()

        @pl.loop(0, chips)
        def _(i):
            both = terms[k, core, i].astype(F32) + halves[k, i].astype(F32)
            paired[k, i] = both.astype(BF16)

        @pl.loop(1, chips)
        def _(step):
            peer = lax.rem(chip + step, chips)
            ring_copy(k, paired.at[k, peer], arrived.at[k, chip], 0, peer, chip).start()

    def scatter_end(k):
        def add(step, total):
            peer = lax.rem(chip + step, chips)
            ring_copy(k, paired.at[k, peer], arrived.at[k, peer], 0, peer, peer).wait_recv()
            return total + arrived[k, peer].astype(F32)

        total = lax.fori_loop(1, chips, add, paired[k, chip].astype(F32))
        whole[k, core, chip] = total.astype(BF16)

        @pl.loop(1, chips)
        def _(step):
            peer = lax.rem(chip + step, chips)
            mine = whole.at[k, core, chip]
            ring_copy(k, mine, mine, 1, peer, chip).start()

    def final_copy(k, side):
        return remote(whole.at[k, side], whole.at[k, side], pair_sem.at[k, 2], pair_sem.at[k, 3], partner)

    def swap_start(k):
        @pl.loop(1, chips)
        def _(step):
            peer = lax.rem(chip + step, chips)
            theirs = whole.at[k, core, peer]
            ring_copy(k, theirs, theirs, 1, peer, peer).wait_recv()

        final_copy(k, core).start()

    def swap_end(k, out):
        final_copy(k, core).wait_send()
        final_copy(k, 1 - core).wait_recv()
        rows = out.shape[0]
        for o in range(n):
            low, high = o * shard, min((o + 1) * shard, rows)
            if low < high:
                out[low:high] = whole[k, o % 2, o // 2, 0 : high - low].astype(F32)

        @pl.loop(1, chips)
        def _(step):
            peer = lax.rem(chip + step, chips)
            ring_copy(k, paired.at[k, peer], arrived.at[k, chip], 0, peer, chip).wait_send()
            mine = whole.at[k, core, chip]
            ring_copy(k, mine, mine, 1, peer, chip).wait_send()

    barrier = pltpu.get_barrier_semaphore()

    @pl.loop(1, n)
    def _(step):
        pl.semaphore_signal(
            barrier,
            inc=1,
            device_id={"mesh": lax.rem(me + step, n)},
            device_id_type=pl.DeviceIdType.MESH,
        )

    targets[1] = mm(mesh_init[...], enc_recv[...]).astype(BF16)
    pl.semaphore_wait(barrier, n - 1)
    first = [
        to_left(0, enc_pack, packs.at[1]),
        to_right(0, enc_pack, packs.at[0]),
        to_left(1, targets.at[1], targets.at[2]),
        to_right(1, targets.at[1], targets.at[0]),
    ]
    for copy in first:
        copy.start()

    values = mm_left_t(grid_in[...], embed_weight[...])
    pre_act[...] = values
    hidden[...] = silu(values).astype(BF16)
    enc_proj[...] = mm(hidden[...], enc_send[...]).astype(BF16)
    dec_target[...] = mm(hidden[...], dec_recv[...]).astype(BF16)

    near_arrive(0, packs.at[0], packs.at[1])
    near_arrive(1, targets.at[0], targets.at[2])

    def enc_tables(k):
        pack, row = ((packs[0], 2), (enc_pack[...], 1), (packs[1], 0))[k]
        return (
            picks(pack[row : row + 1], grid_rows),
            picks(pack[row + 3 : row + 4], mesh_rows),
        )

    for k in range(3):
        source, table = enc_tables(k)
        inputs = mm_left_t(source, enc_proj[...]) + mm_left_t(table, targets[k])
        enc_inputs[k] = inputs
        agg_parts[k] = mm(table, silu(inputs).astype(BF16))
    agg_sends = [
        to_left(2, agg_parts.at[0], agg_near.at[1]),
        to_right(2, agg_parts.at[2], agg_near.at[0]),
    ]
    for copy in agg_sends:
        copy.start()
    near_arrive(2, agg_near.at[0], agg_near.at[1])
    enc_unit, enc_scale = normed(agg_parts[1] + agg_near[0] + agg_near[1])
    latent = (mesh_init[...].astype(F32) + mm(enc_unit.astype(BF16), enc_node[...])).astype(BF16)
    lat_all[me] = latent
    gather_start(0, lat_all)
    mid_target = mm(latent, mid_recv[...]).astype(BF16)
    mid_table = picks(mid_pack[1:2], mesh_rows)
    target_at = mm_left_t(mid_table, mid_target)
    gather_take(0, lat_all, 1, n)
    mid_proj = mm(lat_all[...].reshape(n * mesh_rows, width), mid_send[...]).astype(BF16)
    mid_source = picks(mid_pack[0:1], n * mesh_rows)
    inputs = mm_left_t(mid_source, mid_proj) + target_at
    mid_inputs[...] = inputs
    mid_unit, mid_scale = normed(mm(mid_table, silu(inputs).astype(BF16)))
    mid_norm = (mid_unit * mid_gain[...]).astype(BF16)
    latent_two = (latent.astype(F32) + mm(mid_norm, mid_node[...])).astype(BF16)
    lat2_all[me] = latent_two
    gather_start(1, lat2_all)
    dec_near[1] = mm(latent_two, dec_send[...]).astype(BF16)
    gather_take(1, lat2_all, 1, 2)
    gather_take(1, lat2_all, n - 1, n)
    dec_near[0] = mm(lat2_all[left], dec_send[...]).astype(BF16)
    dec_near[2] = mm(lat2_all[right], dec_send[...]).astype(BF16)

    def dec_forward(j, total):
        source = picks(dec_pack[j, 0:1], mesh_rows)
        table = picks(dec_pack[j, 1:2], grid_rows)
        inputs = mm_left_t(source, dec_near[j]) + mm_left_t(table, dec_target[...])
        dec_inputs[j] = inputs
        return total + mm(table, silu(inputs).astype(BF16))

    dec_agg = lax.fori_loop(0, 3, dec_forward, jnp.zeros((grid_rows, width), F32))
    unit, scale = normed(dec_agg)
    dec_norm = unit.astype(BF16)
    dec_cot[...] = norm_pull(unit, scale, mm_right_t(cotangent[...], dec_node[...])).astype(BF16)
    dec_dst[...] = jnp.zeros((grid_rows, width), F32)

    def dec_backward(j, carry):
        source = picks(dec_pack[j, 0:1], mesh_rows)
        table = picks(dec_pack[j, 1:2], grid_rows)
        grad = (mm_left_t(table, dec_cot[...]) * silu_slope(dec_inputs[j])).astype(BF16)
        dec_parts[j] = mm(source, grad)
        dec_dst[...] += mm(table, grad)
        return carry

    lax.fori_loop(0, 3, dec_backward, 0)
    dec_sends = [
        to_left(3, dec_parts.at[0], dec_back.at[1]),
        to_right(3, dec_parts.at[2], dec_back.at[0]),
    ]
    for copy in dec_sends:
        copy.start()
    put_term(0, mm_left_t(dec_norm, cotangent[...]))
    update[...] = (hidden[...].astype(F32) + mm(dec_norm, dec_node[...])).astype(BF16)
    near_arrive(3, dec_back.at[0], dec_back.at[1])
    dec_src = (dec_parts[1] + dec_back[0] + dec_back[1]).astype(BF16)
    latent_two_grad = mm_right_t(dec_src, dec_send[...])
    grad = mm_right_t(latent_two_grad.astype(BF16), mid_node[...]) * mid_gain[...]
    mid_cot = norm_pull(mid_unit, mid_scale, grad).astype(BF16)
    grad = (mm_left_t(mid_table, mid_cot) * silu_slope(mid_inputs[...])).astype(BF16)
    mid_parts[...] = mm(mid_source, grad).astype(BF16).reshape(n, mesh_rows, width)

    def back_copy(peer, slot):
        return remote(
            mid_parts.at[peer], mid_back.at[slot], all_send.at[2, peer], all_recv.at[2, slot], peer
        )

    @pl.loop(1, n)
    def _(step):
        back_copy(lax.rem(me + step, n), me).start()

    held_dst[...] = mm(mid_table, grad).astype(BF16)
    held_grad[...] = latent_two_grad
    dsg_all[me] = dec_src
    scatter_start(0)

    def back_add(step, total):
        peer = lax.rem(me + step, n)
        back_copy(peer, peer).wait_recv()
        return total + mid_back[peer].astype(F32)

    mid_src = lax.fori_loop(1, n, back_add, mid_parts[me].astype(F32)).astype(BF16)
    msg_all[me] = mid_src
    latent_grad = (
        held_grad[...]
        + mm_right_t(msg_all[me], mid_send[...])
        + mm_right_t(held_dst[...], mid_recv[...])
    ).astype(BF16)
    enc_cot = norm_pull(enc_unit, enc_scale, mm_right_t(latent_grad, enc_node[...])).astype(BF16)
    cots[1] = enc_cot
    cot_sends = [
        to_left(4, cots.at[1], cots.at[2]),
        to_right(4, cots.at[1], cots.at[0]),
    ]
    for copy in cot_sends:
        copy.start()
    gather_start(3, dsg_all)
    gather_start(4, msg_all)
    scatter_end(0)
    near_arrive(4, cots.at[0], cots.at[2])
    enc_src[...] = jnp.zeros((grid_rows, width), F32)
    for k in range(3):
        source, table = enc_tables(k)
        grad = (mm_left_t(table, cots[k]) * silu_slope(enc_inputs[k])).astype(BF16)
        enc_src[...] += mm(source, grad)
    enc_src_grad = enc_src[...].astype(BF16)
    put_term(1, mm_left_t(hidden[...], enc_src_grad))
    hidden_grad = (
        cotangent[...].astype(F32)
        + mm_right_t(enc_src_grad, enc_send[...])
        + mm_right_t(dec_dst[...].astype(BF16), dec_recv[...])
    )
    pre_grad = (hidden_grad * silu_slope(pre_act[...])).astype(BF16)
    put_term(2, mm(grid_in[...], pre_grad))
    scatter_start(1)
    scatter_start(2)
    swap_start(0)
    gather_take(1, lat2_all, 2, n - 1)
    gather_take(3, dsg_all, 1, n)
    gather_take(4, msg_all, 1, n)
    tall = (n * mesh_rows, width)
    decode_grad[...] = mm_left_t(lat2_all[...].reshape(tall), dsg_all[...].reshape(tall))
    process_grad[...] = mm_left_t(lat_all[...].reshape(tall), msg_all[...].reshape(tall))
    swap_end(0, output_grad)
    scatter_end(1)
    scatter_end(2)
    swap_start(1)
    swap_start(2)
    for copy in first + agg_sends + dec_sends + cot_sends:
        copy.wait_send()
    gather_sent(0, lat_all)
    gather_sent(1, lat2_all)
    gather_sent(3, dsg_all)
    gather_sent(4, msg_all)

    @pl.loop(1, n)
    def _(step):
        back_copy(lax.rem(me + step, n), me).wait_send()

    swap_end(1, encode_grad)
    swap_end(2, embed_grad)


def shards(
    grid_in,
    mesh_init,
    embed_weight,
    enc_send,
    enc_recv,
    enc_node,
    mid_send,
    mid_recv,
    mid_node,
    dec_send,
    dec_recv,
    dec_node,
    mid_gain,
    cotangent,
    enc_from,
    enc_into,
    enc_count,
    mid_from,
    mid_into,
    mid_count,
    dec_from,
    dec_into,
    dec_count,
):
    n = lax.axis_size("mesh")
    channels, grid_rows = grid_in.shape
    mesh_rows, width = mesh_init.shape
    span, enc_slots = enc_from.shape
    dec_slots = dec_from.shape[1]
    mid_slots = n * mid_from.shape[1]

    def masked(into, count):
        live = lax.broadcasted_iota(jnp.int32, into.shape, 1) < count[:, None]
        return jnp.where(live, into, -1)

    enc_pack = jnp.concatenate(
        [enc_from, masked(enc_into, enc_count), jnp.zeros((2, enc_slots), jnp.int32)]
    )
    blocks = lax.broadcasted_iota(jnp.int32, mid_from.shape, 0) * mesh_rows
    mid_pack = jnp.stack(
        [(mid_from + blocks).reshape(-1), masked(mid_into, mid_count).reshape(-1)]
    )
    dec_pack = jnp.stack([dec_from, masked(dec_into, dec_count)], axis=1)
    longest = max(width, channels)
    shard = -(-max(16, -(-longest // n)) // 16) * 16
    half = n // 2

    vmem = pltpu.VMEM
    tall = vmem((n, mesh_rows, width), BF16)
    scratch = [
        vmem((grid_rows, width), F32),
        vmem((grid_rows, width), BF16),
        vmem((grid_rows, width), BF16),
        vmem((grid_rows, width), BF16),
        vmem((2,) + enc_pack.shape, jnp.int32),
        vmem((3, mesh_rows, width), BF16),
        vmem((3, enc_slots, width), F32),
        vmem((3, mesh_rows, width), F32),
        vmem((2, mesh_rows, width), F32),
        tall,
        vmem((mid_slots, width), F32),
        tall,
        vmem((3, mesh_rows, width), BF16),
        vmem((3, dec_slots, width), F32),
        vmem((grid_rows, width), BF16),
        vmem((3, mesh_rows, width), F32),
        vmem((2, mesh_rows, width), F32),
        vmem((grid_rows, width), F32),
        tall,
        tall,
        tall,
        tall,
        vmem((3, mesh_rows, width), BF16),
        vmem((grid_rows, width), F32),
        vmem((3, 2, half, shard, width), BF16),
        vmem((3, half, shard, width), BF16),
        vmem((3, half, shard, width), BF16),
        vmem((3, half, shard, width), BF16),
        vmem((3, 2, half, shard, width), BF16),
        vmem((mesh_rows, width), F32),
        vmem((mesh_rows, width), BF16),
        pltpu.SemaphoreType.DMA((5, 2)),
        pltpu.SemaphoreType.DMA((5, 2)),
        pltpu.SemaphoreType.DMA((5, n)),
        pltpu.SemaphoreType.DMA((5, n)),
        pltpu.SemaphoreType.DMA((3, 4)),
        pltpu.SemaphoreType.DMA((3, 2, half)),
        pltpu.SemaphoreType.DMA((3, 2, half)),
    ]
    grad = jax.ShapeDtypeStruct((width, width), F32)
    spec = pl.BlockSpec(memory_space=pltpu.VMEM)
    return pl.pallas_call(
        functools.partial(kernel, n, shard),
        out_shape=(
            jax.ShapeDtypeStruct((grid_rows, width), BF16),
            jax.ShapeDtypeStruct((channels, width), F32),
            grad,
            grad,
            grad,
            grad,
        ),
        in_specs=[spec] * 17,
        out_specs=(spec,) * 6,
        scratch_shapes=scratch,
        compiler_params=pltpu.CompilerParams(
            collective_id=0, has_side_effects=True, vmem_limit_bytes=67043328
        ),
    )(
        grid_in,
        mesh_init,
        embed_weight,
        enc_send,
        enc_recv,
        enc_node,
        mid_send,
        mid_recv,
        mid_node,
        dec_send,
        dec_recv,
        dec_node,
        mid_gain.reshape(1, width),
        cotangent,
        enc_pack,
        mid_pack,
        dec_pack,
    )


def solution(mesh):
    rows = P(("parts", "mesh"), None)
    split = (P("mesh", None), P("mesh", None), P("mesh"))
    return jax.shard_map(
        shards,
        mesh=mesh,
        in_specs=(P(None, ("parts", "mesh")), rows) + (P(),) * 11 + (rows,) + split * 3,
        out_specs=(rows,) + (P("parts", None),) * 5,
        check_vma=False,
    )
```

time: 257 us -> 112 us (0.44)
  waiting for transfers between devices: 161 us -> 0 us
  Pallas kernels: 0 us -> 96.4 us
  matrix products: 40.9 us -> 0 us
  starting transfers between devices: 24.9 us -> 0 us
  between operations: 14.8 us -> 0.68 us
    psum x1 -> x0, waiting for transfers between devices: 119 us -> none  [shards(): lax.psum((embed_term, encode_term, process_term, decode_term, output_term...]
    pallas_call x0 -> x1, Pallas kernels: none -> 96.4 us  [shards(): pl.pallas_call(functools.partial(kernel, n, shard), out_shape=(jax.ShapeD...]
    dot_general x31 -> x0, matrix products: 40.9 us -> none  [the longest x11 10.1 us: mm(): return jnp.dot(left, right, preferred_element_type=jnp.float32)]
    all_to_all x3 -> x0, waiting for transfers between devices: 24.3 us -> none  [the longest x2 18.7 us: send_slots(): lax.all_to_all(block, 'mesh', split_axis=0, concat_axis=0, tiled=True)]
    ppermute x8 -> x0, waiting for transfers between devices: 17.1 us -> none  [the longest x4 11.3 us: shifted(): lax.ppermute(shard, axis, [(i, (i + by) % count) for i in range(count)])]
    all_to_all x3 -> x0, starting transfers between devices: 13.1 us -> none  [the longest x2 7.29 us: send_slots(): lax.all_to_all(block, 'mesh', split_axis=0, concat_axis=0, tiled=True)]
    ppermute x8 -> x0, starting transfers between devices: 11.6 us -> none  [the longest x2 8.24 us: with_halo(): lax.ppermute(head, axis, [((i + 1) % count, i) for i in range(count)])]
    unnamed x139 -> x32, local copies, waits for them, and re-layouts: 10.8 us -> 12.4 us
  transfers between devices with their start and end apart: 12 -> 0, of which waited for: 10 -> 0; matrix products, arithmetic and copies ran while one was open for 6% -> 0% of each run, Pallas kernels for 0% -> 0%
where the time goes in v2:
time: 112 us
  Pallas kernels  96.4 us (86%)
  local copies, waits for them, and re-layouts  12.7 us (11%)
  other arithmetic  2.17 us (2%)
    pallas_call x1, Pallas kernels, shards(): pl.pallas_call(functools.partial(kernel, n, shard), out_shape=(jax.ShapeD...  96.4 us
    unnamed x32, local copies, waits for them, and re-layouts  12.4 us

profile of v2, /device:TPU:0, one launch (start us, length us, event | category | flops | bytes accessed | tf_op | source)
XLA Modules:
  0.0 111.9 jit_solution(12275982924744399959)
XLA Ops:
  0.6 0.0 copy-start.8
  0.7 0.1 pad.6.clone
  0.7 0.0 copy-start.10
  0.7 0.6 copy-done.8
  1.3 0.1 copy-done.10
  1.4 0.0 copy-start.9
  1.4 0.1 fusion.2
  1.5 0.6 copy-done.9
  2.1 0.0 copy-start.4
  2.1 0.7 add_add_fusion.enc_pack
  2.7 0.0 copy-done.4
  2.8 0.0 copy-start.5
  2.8 0.7 copy-done.5
  3.5 0.1 broadcast_add_fusion
  3.5 0.0 copy-start.6
  3.5 0.0 copy-start.11
  3.5 0.1 stack_reshape.6
  3.6 0.6 copy-done.6
  4.2 0.0 copy-done.11
  4.2 0.1 fusion
  4.3 0.0 copy-start.7
  4.3 0.1 stack_reshape.7
  4.4 0.0 copy-start.12
  4.4 0.6 pad_add_fusion.1.mid_pack
  5.0 0.0 copy-done.7
  5.0 0.0 copy-done.12
  5.1 0.1 fusion.1
  5.1 0.6 pad_add_fusion.dec_pack
  5.7 96.4 %shard_map.262 = (bf16[256,512]{1,0:T(8,128)(2,1)}, f32[474,512]{1,0:T(8,128)}, f32[512,512]{1,0:T(8,128)}, f32[512,512]{1,0:T(8,128)}, f32[512,512]{1,0:T(8,128)}, /*index=5*/f32[512,512]{1,0:T(8,128)}) custom-call(bf16[474,256]{1,0:T(8,128)(2,1)} %grid_in.1, bf16[16,512]{1,0:T(8,128)(2,1)} %mesh_init.1, bf16[474,512]{1,0:T(8,128)(2,1)} %embed_weight.1, ...), custom_call_target="tpu_custom_call" | custom-call | tf_op jit(solution)/shard_map/pallas_call | solution.py:533
  102.2 1.7 %copy.35 = bf16[256,512]{1,0:T(8,128)(2,1)} copy(bf16[256,512]{1,0:T(8,128)(2,1)} %get-tuple-element.12) | data formatting | bytes 524288
  103.8 0.0 copy-start.3
  103.8 2.3 %copy.36 = f32[474,512]{1,0:T(8,128)} copy(f32[474,512]{1,0:T(8,128)} %get-tuple-element.13) | data formatting | bytes 1941504
  106.1 0.0 copy-done.3
  106.1 0.0 copy-start.2
  106.1 1.0 copy.37
  107.1 0.6 copy-done.2
  107.7 0.0 copy-start.1
  107.7 1.0 copy.38
  108.7 0.6 copy-done.1
  109.3 0.0 copy-start
  109.3 1.0 copy.39
  110.3 0.6 copy-done
  110.9 1.0 copy.40
  (4 shorter events, 0.0 us)
Async XLA Ops:
  0.6 0.7 copy-start.8
  0.7 0.7 copy-start.10
  1.4 0.7 copy-start.9
  2.1 0.7 copy-start.4
  2.8 0.7 copy-start.5
  3.5 0.7 copy-start.6
  3.5 0.7 copy-start.11
  4.3 0.7 copy-start.7
  4.4 0.7 copy-start.12
  103.8 2.3 %copy-start.3 = (f32[512,512]{1,0:T(8,128)S(1)}, f32[512,512]{1,0:T(8,128)}, u32[]{:S(2)}) copy-start(f32[512,512]{1,0:T(8,128)} %get-tuple-element.14) | copy-start | bytes 3145732
  106.1 1.6 %copy-start.2 = (f32[512,512]{1,0:T(8,128)S(1)}, f32[512,512]{1,0:T(8,128)}, u32[]{:S(2)}) copy-start(f32[512,512]{1,0:T(8,128)} %get-tuple-element.15) | copy-start | bytes 3145732
  107.7 1.6 %copy-start.1 = (f32[512,512]{1,0:T(8,128)S(1)}, f32[512,512]{1,0:T(8,128)}, u32[]{:S(2)}) copy-start(f32[512,512]{1,0:T(8,128)} %get-tuple-element.16) | copy-start | bytes 3145732
  109.3 1.6 %copy-start = (f32[512,512]{1,0:T(8,128)S(1)}, f32[512,512]{1,0:T(8,128)}, u32[]{:S(2)}) copy-start(f32[512,512]{1,0:T(8,128)} %get-tuple-element.17) | copy-start | bytes 3145732

commit v3 on v2

--- a/solution.py
+++ b/solution.py
@@ -74,9 +74,13 @@
     dec_node,
     mid_gain,
     cotangent,
-    enc_pack,
+    enc_from,
+    enc_into,
+    enc_count,
     mid_pack,
-    dec_pack,
+    dec_from,
+    dec_into,
+    dec_count,
     update,
     embed_grad,
     encode_grad,
@@ -88,6 +92,7 @@
     enc_proj,
     dec_target,
     packs,
+    enc_pack,
     targets,
     enc_inputs,
     agg_parts,
@@ -237,7 +242,7 @@
         for o in range(n):
             low, high = o * shard, min((o + 1) * shard, rows)
             if low < high:
-                out[low:high] = whole[k, o % 2, o // 2, 0 : high - low].astype(F32)
+                out[low:high] = whole[k, o % 2, o // 2, 0 : high - low]
 
         @pl.loop(1, chips)
         def _(step):
@@ -257,6 +262,13 @@
             device_id_type=pl.DeviceIdType.MESH,
         )
 
+    def masked(row, count):
+        return jnp.where(lax.broadcasted_iota(jnp.int32, row.shape, 1) < count, row, -1)
+
+    enc_pack[...] = jnp.zeros(enc_pack.shape, jnp.int32)
+    enc_pack[0:3] = enc_from[...]
+    for j in range(3):
+        enc_pack[3 + j : 4 + j] = masked(enc_into[j : j + 1], enc_count[j])
     targets[1] = mm(mesh_init[...], enc_recv[...]).astype(BF16)
     pl.semaphore_wait(barrier, n - 1)
     first = [
@@ -320,8 +332,8 @@
     dec_near[2] = mm(lat2_all[right], dec_send[...]).astype(BF16)
 
     def dec_forward(j, total):
-        source = picks(dec_pack[j, 0:1], mesh_rows)
-        table = picks(dec_pack[j, 1:2], grid_rows)
+        source = picks(dec_from[pl.ds(j, 1)], mesh_rows)
+        table = picks(masked(dec_into[pl.ds(j, 1)], dec_count[j]), grid_rows)
         inputs = mm_left_t(source, dec_near[j]) + mm_left_t(table, dec_target[...])
         dec_inputs[j] = inputs
         return total + mm(table, silu(inputs).astype(BF16))
@@ -333,8 +345,8 @@
     dec_dst[...] = jnp.zeros((grid_rows, width), F32)
 
     def dec_backward(j, carry):
-        source = picks(dec_pack[j, 0:1], mesh_rows)
-        table = picks(dec_pack[j, 1:2], grid_rows)
+        source = picks(dec_from[pl.ds(j, 1)], mesh_rows)
+        table = picks(masked(dec_into[pl.ds(j, 1)], dec_count[j]), grid_rows)
         grad = (mm_left_t(table, dec_cot[...]) * silu_slope(dec_inputs[j])).astype(BF16)
         dec_parts[j] = mm(source, grad)
         dec_dst[...] += mm(table, grad)
@@ -416,8 +428,8 @@
     gather_take(3, dsg_all, 1, n)
     gather_take(4, msg_all, 1, n)
     tall = (n * mesh_rows, width)
-    decode_grad[...] = mm_left_t(lat2_all[...].reshape(tall), dsg_all[...].reshape(tall))
-    process_grad[...] = mm_left_t(lat_all[...].reshape(tall), msg_all[...].reshape(tall))
+    decode_grad[...] = mm_left_t(lat2_all[...].reshape(tall), dsg_all[...].reshape(tall)).astype(BF16)
+    process_grad[...] = mm_left_t(lat_all[...].reshape(tall), msg_all[...].reshape(tall)).astype(BF16)
     swap_end(0, output_grad)
     scatter_end(1)
     scatter_end(2)
@@ -474,14 +486,10 @@
         live = lax.broadcasted_iota(jnp.int32, into.shape, 1) < count[:, None]
         return jnp.where(live, into, -1)
 
-    enc_pack = jnp.concatenate(
-        [enc_from, masked(enc_into, enc_count), jnp.zeros((2, enc_slots), jnp.int32)]
-    )
     blocks = lax.broadcasted_iota(jnp.int32, mid_from.shape, 0) * mesh_rows
     mid_pack = jnp.stack(
         [(mid_from + blocks).reshape(-1), masked(mid_into, mid_count).reshape(-1)]
     )
-    dec_pack = jnp.stack([dec_from, masked(dec_into, dec_count)], axis=1)
     longest = max(width, channels)
     shard = -(-max(16, -(-longest // n)) // 16) * 16
     half = n // 2
@@ -493,7 +501,8 @@
         vmem((grid_rows, width), BF16),
         vmem((grid_rows, width), BF16),
         vmem((grid_rows, width), BF16),
-        vmem((2,) + enc_pack.shape, jnp.int32),
+        vmem((2, 8, enc_slots), jnp.int32),
+        vmem((8, enc_slots), jnp.int32),
         vmem((3, mesh_rows, width), BF16),
         vmem((3, enc_slots, width), F32),
         vmem((3, mesh_rows, width), F32),
@@ -528,19 +537,20 @@
         pltpu.SemaphoreType.DMA((3, 2, half)),
         pltpu.SemaphoreType.DMA((3, 2, half)),
     ]
-    grad = jax.ShapeDtypeStruct((width, width), F32)
+    grad = jax.ShapeDtypeStruct((width, width), BF16)
     spec = pl.BlockSpec(memory_space=pltpu.VMEM)
-    return pl.pallas_call(
+    number = pl.BlockSpec(memory_space=pltpu.SMEM)
+    update, *grads = pl.pallas_call(
         functools.partial(kernel, n, shard),
         out_shape=(
             jax.ShapeDtypeStruct((grid_rows, width), BF16),
-            jax.ShapeDtypeStruct((channels, width), F32),
+            jax.ShapeDtypeStruct((channels, width), BF16),
             grad,
             grad,
             grad,
             grad,
         ),
-        in_specs=[spec] * 17,
+        in_specs=[spec] * 16 + [number] + [spec] * 3 + [number],
         out_specs=(spec,) * 6,
         scratch_shapes=scratch,
         compiler_params=pltpu.CompilerParams(
@@ -561,10 +571,15 @@
         dec_node,
         mid_gain.reshape(1, width),
         cotangent,
-        enc_pack,
+        enc_from,
+        enc_into,
+        enc_count,
         mid_pack,
-        dec_pack,
+        dec_from,
+        dec_into,
+        dec_count,
     )
+    return (update,) + tuple(grad.astype(F32) for grad in grads)
 
 
 def solution(mesh):

time: 112 us -> 106 us (0.946)
  local copies, waits for them, and re-layouts: 12.7 us -> 1.5 us
  other arithmetic: 2.17 us -> 8.01 us
    unnamed x32 -> x15, local copies, waits for them, and re-layouts: 12.4 us -> 1.34 us
    convert_element_type x0 -> x5, other arithmetic: none -> 6.56 us  [shards(): return (update,) + tuple((grad.astype(F32) for grad in grads))]
where the time goes in v3:
time: 106 us
  Pallas kernels  95.7 us (90%)
  other arithmetic  8.01 us (8%)
  local copies, waits for them, and re-layouts  1.5 us (1%)
    pallas_call x1, Pallas kernels, shards(): pl.pallas_call(functools.partial(kernel, n, shard), out_shape=(jax.ShapeD...  95.7 us
    convert_element_type x5, other arithmetic, shards(): return (update,) + tuple((grad.astype(F32) for grad in grads))  6.56 us

profile of v3, /device:TPU:0, one launch (start us, length us, event | category | flops | bytes accessed | tf_op | source)
XLA Modules:
  0.0 105.9 jit_solution(10747043544352873268)
XLA Ops:
  0.6 0.8 broadcast_add_fusion
  1.4 0.0 copy-start.5
  1.4 0.0 copy-start.6
  1.4 0.1 stack_reshape.6
  1.5 0.6 copy-done.5
  2.1 0.0 copy-done.6
  2.1 0.1 fusion
  2.2 0.1 stack_reshape.7
  2.3 0.6 pad_add_fusion.mid_pack
  2.9 95.7 %shard_map.262 = (bf16[256,512]{1,0:T(8,128)(2,1)}, bf16[474,512]{1,0:T(8,128)(2,1)}, bf16[512,512]{1,0:T(8,128)(2,1)}, bf16[512,512]{1,0:T(8,128)(2,1)}, bf16[5...) custom-call(bf16[474,256]{1,0:T(8,128)(2,1)} %grid_in.1, bf16[16,512]{1,0:T(8,128)(2,1)} %mesh_init.1, ...), custom_call_target="tpu_custom_call" | custom-call | tf_op jit(solution)/shard_map/pallas_call | solution.py:543
  98.6 0.0 copy-start.2
  98.6 2.2 %convert_element_type.16 = f32[512,512]{1,0:T(8,128)} convert(bf16[512,512]{1,0:T(8,128)(2,1)} %get-tuple-element.14) | non-fusion elementwise | flops 262144 | bytes 1572864 | tf_op jit(solution)/shard_map/convert_element_type | solution.py:582
  100.8 0.0 copy-done.2
  100.8 0.0 copy-start.1
  100.8 1.1 %convert_element_type.17 = f32[512,512]{1,0:T(8,128)} convert(bf16[512,512]{1,0:T(8,128)(2,1)S(1)} %copy-done.2) | non-fusion elementwise | flops 262144 | bytes 1572864 | tf_op jit(solution)/shard_map/convert_element_type | solution.py:582
  101.9 0.0 copy-done.1
  101.9 0.0 copy-start
  101.9 1.1 %convert_element_type.18 = f32[512,512]{1,0:T(8,128)} convert(bf16[512,512]{1,0:T(8,128)(2,1)S(1)} %copy-done.1) | non-fusion elementwise | flops 262144 | bytes 1572864 | tf_op jit(solution)/shard_map/convert_element_type | solution.py:582
  103.0 0.0 copy-done
  103.0 0.0 copy-start.3
  103.0 1.1 %convert_element_type.19 = f32[512,512]{1,0:T(8,128)} convert(bf16[512,512]{1,0:T(8,128)(2,1)S(1)} %copy-done) | non-fusion elementwise | flops 262144 | bytes 1572864 | tf_op jit(solution)/shard_map/convert_element_type | solution.py:582
  104.1 0.0 copy-done.3
  104.1 0.0 copy-start.4
  104.1 1.1 %convert_element_type.15 = f32[474,512]{1,0:T(8,128)} convert(bf16[474,512]{1,0:T(8,128)(2,1)S(1)} %copy-done.3) | non-fusion elementwise | flops 242688 | bytes 1456128 | tf_op jit(solution)/shard_map/convert_element_type | solution.py:582
  105.2 0.0 copy-done.4
  105.2 0.7 copy.30
  (1 shorter events, 0.0 us)
Async XLA Ops:
  1.4 0.7 copy-start.5
  1.4 0.7 copy-start.6
  98.6 2.2 %copy-start.2 = (bf16[512,512]{1,0:T(8,128)(2,1)S(1)}, bf16[512,512]{1,0:T(8,128)(2,1)}, u32[]{:S(2)}) copy-start(bf16[512,512]{1,0:T(8,128)(2,1)} %get-tuple-element.15) | copy-start | bytes 1572868
  100.8 1.1 %copy-start.1 = (bf16[512,512]{1,0:T(8,128)(2,1)S(1)}, bf16[512,512]{1,0:T(8,128)(2,1)}, u32[]{:S(2)}) copy-start(bf16[512,512]{1,0:T(8,128)(2,1)} %get-tuple-element.16) | copy-start | bytes 1572868
  101.9 1.1 %copy-start = (bf16[512,512]{1,0:T(8,128)(2,1)S(1)}, bf16[512,512]{1,0:T(8,128)(2,1)}, u32[]{:S(2)}) copy-start(bf16[512,512]{1,0:T(8,128)(2,1)} %get-tuple-element.17) | copy-start | bytes 1572868
  103.0 1.1 %copy-start.3 = (bf16[474,512]{1,0:T(8,128)(2,1)S(1)}, bf16[474,512]{1,0:T(8,128)(2,1)}, u32[]{:S(2)}) copy-start(bf16[474,512]{1,0:T(8,128)(2,1)} %get-tuple-element.13) | copy-start | bytes 1456132
  104.1 1.1 %copy-start.4 = (bf16[256,512]{1,0:T(8,128)(2,1)S(1)}, bf16[256,512]{1,0:T(8,128)(2,1)}, u32[]{:S(2)}) copy-start(bf16[256,512]{1,0:T(8,128)(2,1)} %get-tuple-element.24) | copy-start | bytes 786436
